TPU v7x, 256 devices: a whole 4x4x8 slice. The times are simulated.
256 devices in a mesh: expert: 64 (over x, z, core), dp: 4 (over y).
Axes of the slice: x: 4, y: 4, z: 8, core: 2. Of those that a mesh axis runs over, the one named last changes fastest.
Arguments:
- enc_state: bfloat16 [4, 64, 256, 1024], P('dp', 'expert'), may hold values from -6 to 6
- baseline: bfloat16 [4, 64, 256, 1024], P('dp', 'expert'), may hold values from -6 to 6
- enc_keys: bfloat16 [4, 64, 256, 1024], P('dp', 'expert'), may hold values from -4 to 4
- dec_queries: bfloat16 [4, 64, 128, 1024], P('dp', 'expert'), may hold values from -200 to 200
- out_mult: bfloat16 [4, 64, 128, 1024], P('dp', 'expert'), may hold values from -6 to 6
- doc_lengths: int32 [4, 64], P('dp', 'expert'), may hold values from 128 to 256, as said below
- expert_ids: int32 [4, 64, 256], P('dp', 'expert'), may hold values from 0 to 127
- slot_ids: int32 [4, 64, 256], P('dp', 'expert'), may hold values from 0 to 3, as said below
- gate_prob: float32 [4, 64, 256], P('dp', 'expert'), may hold values from 0.2 to 1
- norm_gain: float32 [1024], replicated, may hold values from 0.5 to 2
- w_in: bfloat16 [128, 1024, 2816], P('expert', None, 'dp'), may hold values from -0.1875 to 0.1875
- w_out_t: bfloat16 [128, 1024, 2816], P('expert', None, 'dp'), may hold values from -0.109375 to 0.109375
- w_value: bfloat16 [1024, 1024], replicated, may hold values from -0.1875 to 0.1875
Outputs:
- enc_mult: bfloat16 [4, 64, 256, 1024], P('dp', 'expert')
Inputs may be any that keep to these rules, and one draw needn't show every extreme that they name: `slot_ids`: within one document no two tokens share an expert and a slot, and every token has a slot; one expert has all 4 slots used in every document. `doc_lengths`: some document has all 256 tokens.
All inputs are finite; a program needn't handle non-finite values.
Results may differ from a plain program's by a relative error of at most 0.0069.
Values may be sent and summed in bfloat16 or wider, within the bound.
No kernel may reach another device: no remote copies, remote signals or barrier semaphores. Data moves between devices by JAX's collectives and lax.ppermute only.
A program may use at most 128 MiB of HBM per device.

v0:
```python
import math

import jax
import jax.numpy as jnp
from jax import lax
from jax.sharding import PartitionSpec as P

HEADS = 16
HEAD_DIM = 64


def rescale(pre_act, base_act):
    upper_part = jnp.maximum(jnp.maximum(pre_act, base_act), 0.0)
    lower_part = jnp.maximum(-jnp.minimum(pre_act, base_act), 0.0)
    return upper_part / (upper_part + lower_part + jnp.where(upper_part > 0.0, 0.0, 1.0))


def attend(query_rows, key_rows, mult_rows, length, w_value):
    enc_len = key_rows.shape[0]
    dec_len = query_rows.shape[0]
    queries = query_rows.reshape(dec_len, HEADS, HEAD_DIM)
    keys = key_rows.reshape(enc_len, HEADS, HEAD_DIM)
    mults = mult_rows.reshape(dec_len, HEADS, HEAD_DIM)
    scores = jnp.einsum("qhd,khd->hqk", queries, keys, preferred_element_type=jnp.float32) * (
        1.0 / math.sqrt(HEAD_DIM)
    )
    valid = jnp.arange(enc_len, dtype=jnp.int32) < length
    scores = jnp.where(valid[None, None, :], scores, -jnp.inf)
    top_score = jnp.max(scores, axis=-1, keepdims=True)
    expo = jnp.exp(scores - top_score)
    attn = (expo / jnp.sum(expo, axis=-1, keepdims=True)).astype(jnp.bfloat16)
    value_mult = jnp.einsum("hqk,qhd->khd", attn, mults, preferred_element_type=jnp.float32).astype(
        jnp.bfloat16
    )
    return lax.dot_general(
        value_mult.reshape(enc_len, HEADS * HEAD_DIM),
        w_value,
        (((1,), (1,)), ((), ())),
        preferred_element_type=jnp.float32,
    )


def expert_terms(rows_in, rows_base, rows_mult, part_in, part_out):
    pre_act = jnp.einsum("erd,edf->erf", rows_in, part_in, preferred_element_type=jnp.float32)
    base_act = jnp.einsum("erd,edf->erf", rows_base, part_in, preferred_element_type=jnp.float32)
    hidden_mult = jnp.einsum(
        "erd,edf->erf", rows_mult, part_out, preferred_element_type=jnp.float32
    )
    act_mult = (rescale(pre_act, base_act) * hidden_mult).astype(jnp.bfloat16)
    return jnp.einsum("erf,edf->erd", act_mult, part_in, preferred_element_type=jnp.float32)


def body(
    enc_state,
    baseline,
    enc_keys,
    dec_queries,
    out_mult,
    doc_lengths,
    expert_ids,
    slot_ids,
    gate_prob,
    norm_gain,
    w_in,
    w_out_t,
    w_value,
):
    enc_len = enc_state.shape[2]
    feature_width = enc_state.shape[3]
    local_experts = w_in.shape[0]
    n_experts = local_experts * lax.axis_size("expert")
    capacity = max(2, 2 * enc_len // n_experts)
    tokens = enc_state[0, 0].astype(jnp.float32)
    row_scale = norm_gain * lax.rsqrt(jnp.mean(tokens * tokens, axis=-1, keepdims=True) + 1e-06)
    inputs = (tokens * row_scale).astype(jnp.bfloat16)
    base_inputs = (baseline[0, 0].astype(jnp.float32) * row_scale).astype(jnp.bfloat16)
    flat_slot = expert_ids[0, 0] * capacity + slot_ids[0, 0]
    onehot = (
        flat_slot[None, :] == jnp.arange(n_experts * capacity, dtype=jnp.int32)[:, None]
    ).astype(jnp.bfloat16)

    def dispatch(values):
        placed = jnp.dot(onehot, values, preferred_element_type=jnp.float32).astype(jnp.bfloat16)
        return placed.reshape(n_experts, capacity, feature_width)

    layer_mult = attend(
        dec_queries[0, 0], enc_keys[0, 0], out_mult[0, 0], doc_lengths[0, 0], w_value
    )
    scaled_mult = (gate_prob[0, 0][:, None] * layer_mult).astype(jnp.bfloat16)
    sent_in, sent_base, sent_mult = (
        lax.all_to_all(dispatch(inputs), "expert", split_axis=0, concat_axis=1, tiled=True),
        lax.all_to_all(dispatch(base_inputs), "expert", split_axis=0, concat_axis=1, tiled=True),
        lax.all_to_all(dispatch(scaled_mult), "expert", split_axis=0, concat_axis=1, tiled=True),
    )
    slot_mult = expert_terms(
        sent_in,
        sent_base,
        sent_mult,
        lax.all_gather(w_in, "dp", axis=2, tiled=True),
        lax.all_gather(w_out_t, "dp", axis=2, tiled=True),
    )
    returned = lax.all_to_all(
        slot_mult.astype(jnp.bfloat16), "expert", split_axis=1, concat_axis=0, tiled=True
    )
    per_token = lax.dot_general(
        onehot,
        returned.reshape(n_experts * capacity, feature_width),
        (((0,), (0,)), ((), ())),
        preferred_element_type=jnp.float32,
    )
    result = (layer_mult + row_scale * per_token).astype(jnp.bfloat16)
    return result[None, None]


def solution(mesh):
    in_specs = (
        P("dp", "expert", None, None),
        P("dp", "expert", None, None),
        P("dp", "expert", None, None),
        P("dp", "expert", None, None),
        P("dp", "expert", None, None),
        P("dp", "expert"),
        P("dp", "expert", None),
        P("dp", "expert", None),
        P("dp", "expert", None),
        P(),
        P("expert", None, "dp"),
        P("expert", None, "dp"),
        P(),
    )
    out_specs = P("dp", "expert", None, None)
    return jax.shard_map(body, mesh=mesh, in_specs=in_specs, out_specs=out_specs, check_vma=False)
```

profile of v0, /device:TPU:32, one launch (start us, length us, event | category | flops | bytes accessed | tf_op | source)
XLA Modules:
  0.0 315.6 jit_solution(10270800497459981099)
XLA Ops:
  6.5 0.0 copy-start
  6.5 0.0 copy-start.5
  6.5 0.0 copy-start.9
  6.5 0.0 copy-start.10
  6.5 0.0 copy-start.7
  6.5 0.0 all-gather.3.cloned.1.call-start
  6.6 0.7 all-gather.3.cloned.1.call-update
  7.3 0.0 all-gather.5.cloned.1.call-start
  7.3 0.7 all-gather.5.cloned.1.call-update
  8.0 0.0 copy-done.5
  8.0 0.2 fusion.5
  8.2 0.0 copy-done.9
  8.2 0.0 copy-done.10
  8.3 0.0 copy-done.7
  8.3 0.0 copy-start.6
  8.3 1.6 convolution_convert_fusion.1
  9.9 1.2 reshape.51
  11.2 11.6 %all-to-all-start.1 = ((bf16[128,4,1024]{2,1,0:T(4,128)(2,1)}), bf16[128,4,1024]{2,1,0:T(4,128)(2,1)S(1)}, u32[]{:S(2)}, u32[]{:S(2)}) async-start(bf16[128,4,1024]{2,1,0:T(4,128)(2,1)} %reshape.51), calls=%async_computation.1 | async-start | bytes 2097152 | tf_op jit(solution)/shard_map/all_to_all | solution.py:92
  22.8 2.7 convolution_convert_fusion.2
  25.5 2.4 reshape.50
  27.8 22.8 %all-to-all-done.1 = bf16[128,4,1024]{2,1,0:T(4,128)(2,1)S(1)} async-done(((bf16[128,4,1024]{2,1,0:T(4,128)(2,1)}), bf16[128,4,1024]{2,1,0:T(4,128)(2,1)S(1)}, u32[]{:S(2)}, u32[]{:S(2)}) %all-to-all-start.1) | async-done | bytes 1048608 | tf_op jit(solution)/shard_map/all_to_all | solution.py:92
  50.6 0.0 copy-start.2
  50.6 7.1 %all-to-all-start = ((bf16[128,4,1024]{2,1,0:T(4,128)(2,1)}), bf16[128,4,1024]{2,1,0:T(4,128)(2,1)}, u32[]{:S(2)}, u32[]{:S(2)}) async-start(bf16[128,4,1024]{2,1,0:T(4,128)(2,1)} %reshape.50), calls=%async_computation | async-start | bytes 2097152 | tf_op jit(solution)/shard_map/all_to_all | solution.py:91
  58.4 0.0 copy-done.6
  58.4 0.8 copy.33
  59.2 1.1 copy.35
  60.3 2.0 copy.34
  62.4 3.2 %fusion.29 = (f32[16,128]{1,0:T(8,128)S(1)}, f32[16,128,256]{2,1,0:T(8,128)}) fusion(pred[256]{0:T(512)(128)(4,1)S(1)} %iota_compare_fusion.5, bf16[128,16,64]{0,2,1:T(8,128)(2,1)} %bitcast.64, bf16[256,16,64]{0,2,1:T(8,128)(2,1)} %bitcast.62), kind=kOutput, calls=%fused_computation.47 | convolution fusion | flops 69206272 | bytes 2892032 | tf_op jit(solution)/shard_map/sub | solution.py:30
  65.5 0.0 copy-start.8
  65.5 2.2 convolution_convert_fusion.4
  67.7 0.0 copy-done.2
  67.8 0.0 copy-done
  67.8 0.8 fusion.30
  68.5 0.0 copy-start.3
  68.5 0.0 copy-done.8
  68.6 0.5 convolution_convert_fusion
  69.1 1.2 reshape.52
  70.3 15.2 %all-to-all-done = bf16[128,4,1024]{2,1,0:T(4,128)(2,1)} async-done(((bf16[128,4,1024]{2,1,0:T(4,128)(2,1)}), bf16[128,4,1024]{2,1,0:T(4,128)(2,1)}, u32[]{:S(2)}, u32[]{:S(2)}) %all-to-all-start) | async-done | bytes 1048608 | tf_op jit(solution)/shard_map/all_to_all | solution.py:91
  85.5 6.9 %all-to-all-start.2 = ((bf16[128,4,1024]{2,1,0:T(4,128)(2,1)}), bf16[128,4,1024]{2,1,0:T(4,128)(2,1)S(1)}, u32[]{:S(2)}, u32[]{:S(2)}) async-start(bf16[128,4,1024]{2,1,0:T(4,128)(2,1)} %reshape.52), calls=%async_computation.2 | async-start | bytes 2097152 | tf_op jit(solution)/shard_map/all_to_all | solution.py:93
  92.4 0.0 copy-done.3
  92.4 1.4 copy.48
  93.8 2.2 all_to_all.57
  96.0 1.6 copy.49
  97.6 1.1 all_to_all.53
  98.7 21.6 %all-to-all-done.2 = bf16[128,4,1024]{2,1,0:T(4,128)(2,1)S(1)} async-done(((bf16[128,4,1024]{2,1,0:T(4,128)(2,1)}), bf16[128,4,1024]{2,1,0:T(4,128)(2,1)S(1)}, u32[]{:S(2)}, u32[]{:S(2)}) %all-to-all-start.2) | async-done | bytes 1048608 | tf_op jit(solution)/shard_map/all_to_all | solution.py:93
  120.3 1.1 copy.38
  121.3 0.0 copy-start.4
  121.4 2.8 all-gather.3.cloned.1.call-done
  124.1 10.3 %fusion.31 = f32[2,256,2816]{2,1,0:T(8,128)} fusion(bf16[2,256,1024]{2,1,0:T(8,128)(2,1)} %all_to_all.53, bf16[2,1024,2816]{1,2,0:T(8,128)(2,1)} %all-gather.3.cloned.1.call-done), kind=kOutput, calls=%fused_computation.49 | convolution fusion | flops 2952790016 | bytes 18350080 | tf_op jit(solution)/shard_map/erd,edf->erf/dot_general | solution.py:44
  134.4 0.0 copy-done.4
  134.4 13.9 %fusion.32 = f32[2,256,2816]{2,1,0:T(8,128)} fusion(bf16[2,256,1024]{2,1,0:T(8,128)(2,1)S(1)} %copy-done.4, bf16[2,1024,2816]{1,2,0:T(8,128)(2,1)} %all-gather.3.cloned.1.call-done), kind=kOutput, calls=%fused_computation.50 | convolution fusion | flops 2952790016 | bytes 18350080 | tf_op jit(solution)/shard_map/erd,edf->erf/dot_general | solution.py:45
  148.3 91.0 %all-gather.5.cloned.1.call-done = bf16[2,1024,2816]{1,2,0:T(8,128)(2,1)} async-done(((bf16[2,1024,704]{1,2,0:T(8,128)(2,1)}), bf16[2,1024,2816]{1,2,0:T(8,128)(2,1)}) %all-gather.5.cloned.1.call-update) | async-done | bytes 11534352 | tf_op jit(solution)/shard_map/all_gather | solution.py:100
  239.3 15.6 %multiply_convert_fusion = bf16[2,256,2816]{2,1,0:T(8,128)(2,1)} fusion(f32[2,256,2816]{2,1,0:T(8,128)} %fusion.31, f32[2,256,2816]{2,1,0:T(8,128)} %fusion.32, bf16[2,1024,2816]{1,2,0:T(8,128)(2,1)} %all-gather.5.cloned.1.call-done, bf16[2,256,1024]{2,0,1:T(2,128)(2,1)S(1)} %bitcast.60), kind=kOutput, calls=%fused_computation.1 | convolution fusion | flops 2970091520 | bytes 27000832 | tf_op jit(solution)/shard_map/erd,edf->erf/dot_general | solution.py:46
  254.9 0.0 copy-start.1
  254.9 8.4 %convolution_convert_fusion.3 = bf16[2,256,1024]{2,1,0:T(8,128)(2,1)S(1)} fusion(bf16[2,256,2816]{2,1,0:T(8,128)(2,1)} %multiply_convert_fusion, bf16[2,1024,2816]{1,2,0:T(8,128)(2,1)} %all-gather.3.cloned.1.call-done), kind=kOutput, calls=%fused_computation.12 | convolution fusion | flops 2953314304 | bytes 15466496 | tf_op jit(solution)/shard_map/erf,edf->erd/dot_general | solution.py:50
  263.3 1.1 copy.40
  264.4 38.1 %all_to_all.69 = bf16[2,256,1024]{2,0,1:T(2,128)(2,1)S(1)} all-to-all(bf16[2,256,1024]{2,0,1:T(2,128)(2,1)S(1)} %copy.40), channel_id=1, replica_groups=mesh['expert'=64,'dp'=4] {'expert'}, dimensions={1} | all-to-all | bytes 2097152 | tf_op jit(solution)/shard_map/all_to_all | solution.py:102
  302.6 1.5 copy.47
  304.1 2.2 reshape.53
  306.2 2.5 fusion.4
  308.7 0.0 copy-done.1
  (3 shorter events, 0.0 us)
Async XLA Ops:
  6.5 61.2 %copy-start = (bf16[1024,1024]{1,0:T(8,128)(2,1)S(1)}, bf16[1024,1024]{1,0:T(8,128)(2,1)}, u32[]{:S(2)}) copy-start(bf16[1024,1024]{1,0:T(8,128)(2,1)} %param.25) | copy-start | bytes 6291460
  6.5 1.5 copy-start.5
  6.5 1.7 copy-start.9
  6.5 1.7 copy-start.10
  6.5 1.7 copy-start.7
  6.5 117.6 %all-gather.3.cloned.1.call-start = ((), (), s32[]{:S(2)}) async-start(), calls=%async_computation.4 | async-start | bytes 14417920 | tf_op jit(solution)/shard_map/all_gather | solution.py:99
  7.3 232.0 %all-gather.5.cloned.1.call-start = ((), (), s32[]{:S(2)}) async-start(), calls=%async_computation.5 | async-start | bytes 14417920 | tf_op jit(solution)/shard_map/all_gather | solution.py:100
  8.3 50.1 %copy-start.6 = (bf16[1,1,128,1024]{3,2,1,0:T(8,128)(2,1)S(1)}, bf16[1,1,128,1024]{3,2,1,0:T(8,128)(2,1)}, u32[]{:S(2)}) copy-start(bf16[1,1,128,1024]{3,2,1,0:T(8,128)(2,1)} %param.16) | copy-start | bytes 786436
  11.2 39.5 %all-to-all-start.1 = ((bf16[128,4,1024]{2,1,0:T(4,128)(2,1)}), bf16[128,4,1024]{2,1,0:T(4,128)(2,1)S(1)}, u32[]{:S(2)}, u32[]{:S(2)}) async-start(bf16[128,4,1024]{2,1,0:T(4,128)(2,1)} %reshape.51), calls=%async_computation.1 | async-start | bytes 2097152 | tf_op jit(solution)/shard_map/all_to_all | solution.py:92
  50.6 17.1 %copy-start.2 = (bf16[128,4,1024]{2,1,0:T(4,128)(2,1)}, bf16[128,4,1024]{2,1,0:T(4,128)(2,1)S(1)}, u32[]{:S(2)}) copy-start(bf16[128,4,1024]{2,1,0:T(4,128)(2,1)S(1)} %all-to-all-done.1) | copy-start | bytes 3145732
  50.6 34.9 %all-to-all-start = ((bf16[128,4,1024]{2,1,0:T(4,128)(2,1)}), bf16[128,4,1024]{2,1,0:T(4,128)(2,1)}, u32[]{:S(2)}, u32[]{:S(2)}) async-start(bf16[128,4,1024]{2,1,0:T(4,128)(2,1)} %reshape.50), calls=%async_computation | async-start | bytes 2097152 | tf_op jit(solution)/shard_map/all_to_all | solution.py:91
  65.5 3.0 copy-start.8
  68.5 23.9 %copy-start.3 = (bf16[128,4,1024]{2,1,0:T(4,128)(2,1)S(1)}, bf16[128,4,1024]{2,1,0:T(4,128)(2,1)}, u32[]{:S(2)}) copy-start(bf16[128,4,1024]{2,1,0:T(4,128)(2,1)} %copy-done.2) | copy-start | bytes 3145732
  85.5 34.8 %all-to-all-start.2 = ((bf16[128,4,1024]{2,1,0:T(4,128)(2,1)}), bf16[128,4,1024]{2,1,0:T(4,128)(2,1)S(1)}, u32[]{:S(2)}, u32[]{:S(2)}) async-start(bf16[128,4,1024]{2,1,0:T(4,128)(2,1)} %reshape.52), calls=%async_computation.2 | async-start | bytes 2097152 | tf_op jit(solution)/shard_map/all_to_all | solution.py:93
  121.3 13.1 %copy-start.4 = (bf16[2,256,1024]{2,1,0:T(8,128)(2,1)S(1)}, bf16[2,256,1024]{2,1,0:T(8,128)(2,1)}, u32[]{:S(2)}) copy-start(bf16[2,256,1024]{2,1,0:T(8,128)(2,1)} %all_to_all.57) | copy-start | bytes 3145732
  254.9 53.9 %copy-start.1 = (bf16[1024,1024]{1,0:T(8,128)(2,1)S(1)}, bf16[1024,1024]{1,0:T(8,128)(2,1)}, u32[]{:S(2)}) copy-start(bf16[1024,1024]{1,0:T(8,128)(2,1)} %param.25) | copy-start | bytes 6291460
Sparse Core Ops, SparseCore 0:
  9.2 114.8 all-gather.2
  125.9 113.2 all-gather.4
where the time goes:
time: 318 us; the launch traced here: 316 us
  waiting for transfers between devices  155 us (49%)
  matrix products  61.7 us (19%)
  blocking collectives  38.1 us (12%)
  starting transfers between devices  25.6 us (8%)
  local copies, waits for them, and re-layouts  21 us (7%)
  between operations  14.3 us (4%)
    all_gather x1, waiting for transfers between devices, body(): lax.all_gather(w_out_t, 'dp', axis=2, tiled=True)  91 us
    all_to_all x1, blocking collectives, body(): lax.all_to_all(slot_mult.astype(jnp.bfloat16), 'expert', split_axis=1, co...  38.1 us
    all_to_all x1, waiting for transfers between devices, body(): lax.all_to_all(dispatch(base_inputs), 'expert', split_axis=0, concat_axis...  22.8 us
    all_to_all x1, waiting for transfers between devices, body(): lax.all_to_all(dispatch(scaled_mult), 'expert', split_axis=0, concat_axis...  21.6 us
    dot_general x1, matrix products, expert_terms(): jnp.einsum('erd,edf->erf', rows_mult, part_out, preferred_element_type=jn...  15.6 us
    all_to_all x1, waiting for transfers between devices, body(): lax.all_to_all(dispatch(inputs), 'expert', split_axis=0, concat_axis=1, t...  15.2 us
    dot_general x1, matrix products, expert_terms(): jnp.einsum('erd,edf->erf', rows_base, part_in, preferred_element_type=jnp...  13.9 us
    all_to_all x1, starting transfers between devices, body(): lax.all_to_all(dispatch(base_inputs), 'expert', split_axis=0, concat_axis...  11.6 us
  transfers between devices with their start and end apart: 5, of which 5 were waited for; matrix products, arithmetic and copies ran while one was open for 15% of the time, Pallas kernels for 0%

commit v1 on v0

v1 whole, which is shorter than its diff:
```python
import math

import jax
import jax.numpy as jnp
from jax import lax
from jax.experimental import pallas as pl
from jax.experimental.pallas import tpu as pltpu
from jax.sharding import PartitionSpec as P

HEAD_DIM = 64
NT = (((1,), (1,)), ((), ()))
F32 = jnp.float32
BF16 = jnp.bfloat16


def mm(lhs, rhs):
    return jnp.dot(lhs, rhs, preferred_element_type=F32)


def mm_nt(lhs, rhs):
    return lax.dot_general(lhs, rhs, NT, preferred_element_type=F32)


def column_of(row):
    n = row.shape[1]
    eye = lax.broadcasted_iota(jnp.int32, (n, n), 0) == lax.broadcasted_iota(jnp.int32, (n, n), 1)
    return jnp.sum(jnp.where(eye, jnp.broadcast_to(row, (n, n)), 0.0), axis=1, keepdims=True)


def prepare_kernel(
    length_ref, ids_ref, slots_ref, gate_ref, gain_ref, enc_hbm, base_hbm, keys_hbm, query_hbm, mult_hbm, wv_hbm,
    placed_ref, layer_ref, scale_ref,
    enc_ref, base_ref, keys_ref, query_ref, mult_ref, wv_ref, value_ref, sems,
):
    enc_len, width = enc_ref.shape
    dec_len = query_ref.shape[0]
    copies = [
        pltpu.make_async_copy(src, dst, sems.at[i])
        for i, (src, dst) in enumerate(
            (
                (keys_hbm, keys_ref), (query_hbm, query_ref), (mult_hbm, mult_ref),
                (wv_hbm, wv_ref), (enc_hbm, enc_ref), (base_hbm, base_ref),
            )
        )
    ]
    for copy in copies:
        copy.start()
    for copy in copies[:3]:
        copy.wait()
    first = lax.broadcasted_iota(jnp.int32, (dec_len, 2 * HEAD_DIM), 1) < HEAD_DIM
    valid = lax.broadcasted_iota(jnp.int32, (enc_len, 2 * dec_len), 0) < length_ref[0, 0]
    for pair in range(width // (2 * HEAD_DIM)):
        lanes = slice(pair * 2 * HEAD_DIM, (pair + 1) * 2 * HEAD_DIM)
        query, mult = query_ref[:, lanes], mult_ref[:, lanes]
        zeros = jnp.zeros_like(query)
        queries = jnp.concatenate([jnp.where(first, query, zeros), jnp.where(first, zeros, query)], axis=0)
        mults = jnp.concatenate([jnp.where(first, mult, zeros), jnp.where(first, zeros, mult)], axis=0)
        scores = mm_nt(keys_ref[:, lanes], queries) * (1.0 / math.sqrt(HEAD_DIM))
        scores = jnp.where(valid, scores, -jnp.inf)
        expo = jnp.exp(scores - jnp.max(scores, axis=0, keepdims=True))
        attn = (expo * (1.0 / jnp.sum(expo, axis=0, keepdims=True))).astype(BF16)
        value_ref[:, lanes] = mm(attn, mults).astype(BF16)
    copies[3].wait()
    layer_mult = mm_nt(value_ref[...], wv_ref[...])
    layer_ref[...] = layer_mult
    scaled_mult = (column_of(gate_ref[...]) * layer_mult).astype(BF16)
    copies[4].wait()
    copies[5].wait()
    tokens = enc_ref[...].astype(F32)
    inv = lax.rsqrt(jnp.mean(tokens * tokens, axis=-1, keepdims=True) + 1e-06)
    scale_ref[...] = jnp.broadcast_to(inv, scale_ref.shape)
    row_scale = gain_ref[...] * inv
    inputs = (tokens * row_scale).astype(BF16)
    base_inputs = (base_ref[...].astype(F32) * row_scale).astype(BF16)
    half = width // 2
    row = ids_ref[...] * 8 + slots_ref[...]
    at = lax.broadcasted_iota(jnp.int32, (placed_ref.shape[0], enc_len), 0)
    low = jnp.where(at == row, 1.0, 0.0).astype(BF16)
    high = jnp.where(at == row + 4, 1.0, 0.0).astype(BF16)
    placed_ref[:, :half] = (mm(low, inputs[:, :half]) + mm(high, inputs[:, half:])).astype(BF16)
    placed_ref[:, half:width] = (mm(low, base_inputs[:, :half]) + mm(high, base_inputs[:, half:])).astype(BF16)
    placed_ref[:, width:] = (mm(low, scaled_mult[:, :half]) + mm(high, scaled_mult[:, half:])).astype(BF16)


def prepare(length, ids, slots, gate, gain, enc, base, keys, query, mult, wv, n_rows):
    enc_len, width = enc.shape
    any_spec = pl.BlockSpec(memory_space=pl.ANY)
    vmem = pl.BlockSpec(memory_space=pltpu.VMEM)
    return pl.pallas_call(
        prepare_kernel,
        in_specs=[pl.BlockSpec(memory_space=pltpu.SMEM)] + [vmem] * 4 + [any_spec] * 6,
        out_specs=[vmem] * 3,
        out_shape=[
            jax.ShapeDtypeStruct((n_rows, 3 * width // 2), BF16),
            jax.ShapeDtypeStruct((enc_len, width), F32),
            jax.ShapeDtypeStruct((enc_len, 128), F32),
        ],
        scratch_shapes=[pltpu.VMEM(a.shape, BF16) for a in (enc, base, keys, query, mult, wv)]
        + [pltpu.VMEM((enc_len, width), BF16), pltpu.SemaphoreType.DMA((6,))],
        compiler_params=pltpu.CompilerParams(vmem_limit_bytes=48 << 20),
        name="prepare",
    )(length, ids, slots, gate, gain, enc, base, keys, query, mult, wv)


def expert_kernel(rows_ref, *refs, n_parts):
    weights_hbm = refs[: 2 * n_parts]
    out_ref = refs[2 * n_parts]
    weights = refs[2 * n_parts + 1 : 4 * n_parts + 1]
    in_ref, base_ref, mult_ref, acc_ref, sems = refs[4 * n_parts + 1 :]
    copies = [
        pltpu.make_async_copy(weights_hbm[i], weights[i], sems.at[i]) for i in range(2 * n_parts)
    ]
    for copy in copies:
        copy.start()
    n_tiles, _, lanes = rows_ref.shape
    half = lanes // 3
    upper_rows = lax.broadcasted_iota(jnp.int32, (n_tiles // 2, 8, half), 1) < 4
    for i, ref in enumerate((in_ref, base_ref, mult_ref)):
        block = rows_ref[:, :, i * half : (i + 1) * half].astype(F32).reshape(n_tiles // 2, 2, 8, half)
        even, odd = block[:, 0], block[:, 1]
        low = jnp.where(upper_rows, even, pltpu.roll(odd, 4, 1))
        high = jnp.where(upper_rows, pltpu.roll(even, 4, 1), odd)
        ref[:, :half] = low.reshape(n_tiles * 4, half).astype(BF16)
        ref[:, half:] = high.reshape(n_tiles * 4, half).astype(BF16)
    n_rows = n_tiles * 4
    block = n_rows // 2
    for part in range(n_parts):
        copies[2 * part].wait()
        copies[2 * part + 1].wait()
        part_in, part_out = weights[2 * part], weights[2 * part + 1]
        for at in range(0, n_rows, block):
            rows = slice(at, at + block)
            pre_act = mm(in_ref[rows, :], part_in[...])
            base_act = mm(base_ref[rows, :], part_in[...])
            hidden_mult = mm(mult_ref[rows, :], part_out[...])
            upper_part = jnp.maximum(jnp.maximum(pre_act, base_act), 0.0)
            lower_part = jnp.maximum(-jnp.minimum(pre_act, base_act), 0.0)
            ratio = upper_part / (upper_part + lower_part + jnp.where(upper_part > 0.0, 0.0, 1.0))
            term = mm_nt((ratio * hidden_mult).astype(BF16), part_in[...])
            if part == 0:
                acc_ref[rows, :] = term
            else:
                acc_ref[rows, :] += term
    low = acc_ref[:, :half].reshape(n_tiles // 2, 8, half)
    high = acc_ref[:, half:].reshape(n_tiles // 2, 8, half)
    even = jnp.where(upper_rows, low, pltpu.roll(high, 4, 1)).astype(BF16)
    odd = jnp.where(upper_rows, pltpu.roll(low, 4, 1), high).astype(BF16)
    out_ref[:, 0] = even
    out_ref[:, 1] = odd


def expert_terms(rows, parts):
    n_tiles, _, lanes = rows.shape
    half = lanes // 3
    flat = [w for pair in parts for w in pair]
    out = pl.pallas_call(
        lambda *refs: expert_kernel(*refs, n_parts=len(parts)),
        in_specs=[pl.BlockSpec(memory_space=pltpu.VMEM)] + [pl.BlockSpec(memory_space=pl.ANY)] * len(flat),
        out_specs=pl.BlockSpec(memory_space=pltpu.VMEM),
        out_shape=jax.ShapeDtypeStruct((n_tiles // 2, 2, 8, half), BF16),
        scratch_shapes=[pltpu.VMEM(w.shape, BF16) for w in flat]
        + [pltpu.VMEM((n_tiles * 4, 2 * half), BF16)] * 3
        + [pltpu.VMEM((n_tiles * 4, 2 * half), F32), pltpu.SemaphoreType.DMA((len(flat),))],
        compiler_params=pltpu.CompilerParams(vmem_limit_bytes=56 << 20),
        name="expert",
    )(rows, *flat)
    return out.reshape(n_tiles, 8, half)


def combine_kernel(ids_ref, slots_ref, gain_ref, scale_ref, layer_ref, back_ref, out_ref):
    enc_len, width = layer_ref.shape
    half = width // 2
    row = column_of((ids_ref[...] * 8 + slots_ref[...]).astype(F32)).astype(jnp.int32)
    at = lax.broadcasted_iota(jnp.int32, (enc_len, back_ref.shape[0]), 1)
    row_scale = gain_ref[...] * scale_ref[:, :1]
    for i in range(2):
        lanes = slice(i * half, (i + 1) * half)
        chosen = jnp.where(at == row + 4 * i, 1.0, 0.0).astype(BF16)
        per_token = mm(chosen, back_ref[...])
        out_ref[:, lanes] = (layer_ref[:, lanes] + row_scale[:, lanes] * per_token).astype(BF16)


def combine(ids, slots, gain, scale, layer_mult, back):
    return pl.pallas_call(
        combine_kernel,
        in_specs=[pl.BlockSpec(memory_space=pltpu.VMEM)] * 6,
        out_specs=pl.BlockSpec(memory_space=pltpu.VMEM),
        out_shape=jax.ShapeDtypeStruct(layer_mult.shape, BF16),
        compiler_params=pltpu.CompilerParams(vmem_limit_bytes=32 << 20),
        name="combine",
    )(ids, slots, gain, scale, layer_mult, back)


def exchange_weights(w_in, w_out_t, n_expert_devices):
    axes = ("expert", "dp")
    dp_at = lax.axis_index("dp")
    pieces = []
    for step in range(2):
        pairs = []
        for chip in range(n_expert_devices // 2):
            for core in range(2):
                for part in range(4):
                    own = (part // 2 + step) % 2
                    to_dp, to_core = 2 * core + own, part % 2
                    pairs.append(((chip * 2 + core) * 4 + part, (chip * 2 + to_core) * 4 + to_dp))
        own = (dp_at // 2 + step) % 2
        for weights in (w_in, w_out_t):
            sent = lax.dynamic_index_in_dim(weights, own, 0, keepdims=False)
            pieces.append(lax.ppermute(sent, axes, pairs))
    swap = [(i, i ^ 1) for i in range(n_expert_devices)]
    swapped = [lax.ppermute(piece, "expert", swap) for piece in pieces]
    both = pieces + swapped
    return list(zip(both[0::2], both[1::2]))


def body(
    enc_state, baseline, enc_keys, dec_queries, out_mult, doc_lengths, expert_ids, slot_ids, gate_prob, norm_gain,
    w_in, w_out_t, w_value,
):
    enc_len, width = enc_state.shape[2:]
    n_expert_devices = lax.axis_size("expert")
    n_experts = w_in.shape[0] * n_expert_devices
    axes = ("expert", "dp")
    groups = [
        [(chip * 2 + core) * 4 + at for chip in range(n_expert_devices // 2) for at in range(4)] for core in range(2)
    ]

    def exchange(rows):
        return lax.all_to_all(rows, axes, split_axis=0, concat_axis=0, axis_index_groups=groups, tiled=True)

    parts = exchange_weights(w_in, w_out_t, n_expert_devices)
    ids, slots, gain = expert_ids[0], slot_ids[0], norm_gain[None, :]
    placed, layer_mult, scale = prepare(
        doc_lengths, ids, slots, gate_prob[0], gain, enc_state[0, 0], baseline[0, 0], enc_keys[0, 0],
        dec_queries[0, 0], out_mult[0, 0], w_value, n_experts * 8,
    )
    came = exchange(placed.reshape(n_experts, 8, 3 * width // 2))
    slot_mult = expert_terms(came, parts)
    back = exchange(slot_mult)
    result = combine(ids, slots, gain, scale, layer_mult, back.reshape(n_experts * 8, width // 2))
    return result[None, None]


def solution(mesh):
    rows = P("dp", "expert", None)
    in_specs = (P("dp", "expert", None, None),) * 5 + (P("dp", "expert"),) + (rows,) * 3 + (
        P(), P("expert", None, "dp"), P("expert", None, "dp"), P(),
    )
    out_specs = P("dp", "expert", None, None)
    return jax.shard_map(body, mesh=mesh, in_specs=in_specs, out_specs=out_specs, check_vma=False)
```

time: 318 us -> 215 us (0.68)
  waiting for transfers between devices: 155 us -> 3.38 us
  starting transfers between devices: 25.6 us -> 111 us
  matrix products: 61.7 us -> 0 us
  Pallas kernels: 0 us -> 27.8 us
  between operations: 14.3 us -> 0.83 us
  local copies, waits for them, and re-layouts: 21 us -> 31.5 us
    ppermute x0 -> x8, starting transfers between devices: none -> 95.4 us  [the longest x4 86.7 us: exchange_weights(): swapped = [lax.ppermute(piece, 'expert', swap) for piece in pieces]]
    all_gather x2 -> x0, waiting for transfers between devices: 93.7 us -> none  [the longest x1 91 us: body(): lax.all_gather(w_out_t, 'dp', axis=2, tiled=True)]
    all_to_all x3 -> x1, waiting for transfers between devices: 59.6 us -> 0.01 us  [exchange(): lax.all_to_all(rows, axes, split_axis=0, concat_axis=0, axis_index_groups...]
    dot_general x10 -> x0, matrix products: 58.5 us -> none  [the longest x1 15.6 us: expert_terms(): jnp.einsum('erd,edf->erf', rows_mult, part_out, preferred_element_type=jn...]
    pallas_call x0 -> x3, Pallas kernels: none -> 27.8 us  [the longest x1 20 us: expert_terms(): pl.pallas_call(lambda *refs: expert_kernel(*refs, n_parts=len(parts)), in...]
    ppermute x0 -> x8, local copies, waits for them, and re-layouts: none -> 19.7 us  [the longest x4 10.3 us: exchange_weights(): swapped = [lax.ppermute(piece, 'expert', swap) for piece in pieces]]
    all_to_all x3 -> x1, starting transfers between devices: 25.5 us -> 15.4 us  [exchange(): lax.all_to_all(rows, axes, split_axis=0, concat_axis=0, axis_index_groups...]
    all_to_all x6 -> x0, local copies, waits for them, and re-layouts: 8.89 us -> none  [the longest x2 3.57 us: body(): lax.all_to_all(dispatch(base_inputs), 'expert', split_axis=0, concat_axis...]
  transfers between devices with their start and end apart: 5 -> 9, of which waited for: 5 -> 1; matrix products, arithmetic and copies ran while one was open for 15% -> 10% of each run, Pallas kernels for 0% -> 0%
where the time goes in v1:
time: 215 us; the launch traced here: 214 us
  starting transfers between devices  111 us (52%)
  blocking collectives  39.7 us (18%)
  local copies, waits for them, and re-layouts  31.5 us (15%)
  Pallas kernels  27.8 us (13%)
  waiting for transfers between devices  3.38 us (2%)
    ppermute x4, starting transfers between devices, exchange_weights(): swapped = [lax.ppermute(piece, 'expert', swap) for piece in pieces]  86.7 us
    all_to_all x1, blocking collectives, exchange(): lax.all_to_all(rows, axes, split_axis=0, concat_axis=0, axis_index_groups...  39.7 us
    pallas_call x1, Pallas kernels, expert_terms(): pl.pallas_call(lambda *refs: expert_kernel(*refs, n_parts=len(parts)), in...  20 us
    all_to_all x1, starting transfers between devices, exchange(): lax.all_to_all(rows, axes, split_axis=0, concat_axis=0, axis_index_groups...  15.4 us
    ppermute x4, local copies, waits for them, and re-layouts, exchange_weights(): swapped = [lax.ppermute(piece, 'expert', swap) for piece in pieces]  10.3 us
    unnamed x28, local copies, waits for them, and re-layouts  9.35 us
    ppermute x4, local copies, waits for them, and re-layouts, exchange_weights(): pieces.append(lax.ppermute(sent, axes, pairs))  9.34 us
    ppermute x4, starting transfers between devices, exchange_weights(): pieces.append(lax.ppermute(sent, axes, pairs))  8.72 us
  transfers between devices with their start and end apart: 9, of which 1 were waited for; matrix products, arithmetic and copies ran while one was open for 10% of the time, Pallas kernels for 0%

profile of v1, /device:TPU:32, one launch (start us, length us, event | category | flops | bytes accessed | tf_op | source)
XLA Modules:
  0.0 214.1 jit_solution(11564596197594670330)
XLA Ops:
  0.7 0.0 copy-start
  0.7 1.6 copy-done
  2.2 0.0 copy-start.1
  2.2 1.0 copy-done.1
  3.3 0.0 copy-start.2
  3.3 1.0 copy-done.2
  4.3 0.0 copy-start.3
  4.3 1.0 copy-done.3
  5.4 0.0 copy-start.4
  5.4 0.9 copy-done.4
  6.3 0.0 copy-start.5
  6.3 0.9 copy-done.5
  7.3 0.0 copy-start.6
  7.3 0.7 copy-done.6
  8.0 0.0 copy-start.8
  8.0 0.7 copy-done.8
  8.6 0.0 copy-start.10
  8.6 0.7 copy-done.10
  9.3 0.0 copy-start.12
  9.3 0.7 copy-done.12
  10.0 6.2 %prepare.1 = (bf16[1024,1536]{1,0:T(8,128)(2,1)}, f32[256,1024]{1,0:T(8,128)S(1)}, f32[256,128]{1,0:T(8,128)S(1)}) custom-call(s32[1,1]{1,0:T(1,128)S(6)} %copy.26.length_ref, s32[1,256]{1,0:T(1,128)S(1)} %bitcast.29, s32[1,256]{1,0:T(1,128)S(1)} %bitcast.31, f32[1,256]{1,0:T(1,128)S(1)} %bitcast.33, f32[1,1024]{1,0:T(1,128)S(1)} %bitcast.27, ...), custom_call_target="tpu_custom_call" | custom-call | tf_op jit(solution)/shard_map/prepare/pallas_call | solution.py:89
  16.2 15.4 %all-to-all-start = ((bf16[128,8,1536]{2,1,0:T(8,128)(2,1)}), bf16[128,8,1536]{2,1,0:T(8,128)(2,1)}, u32[]{:S(2)}, u32[]{:S(2)}) async-start(bf16[128,8,1536]{2,1,0:T(8,128)(2,1)} %bitcast.35), calls=%async_computation | async-start | bytes 6291456 | tf_op jit(solution)/shard_map/all_to_all | solution.py:229
  31.7 0.0 copy-start.13
  31.7 2.2 %dynamic-slice_bitcast_fusion.1 = (bf16[1024,704]{0,1:T(8,128)(2,1)S(1)}, bf16[1024,704]{0,1:T(8,128)(2,1)S(1)}) fusion(bf16[2,1024,704]{1,2,0:T(8,128)(2,1)} %param.23, s32[]{:T(128)S(6)} %select_n.29, s32[]{:T(128)S(6)} %select_n.27), kind=kLoop, calls=%fused_computation.1 | loop fusion | bytes 5767176 | tf_op jit(solution)/shard_map/jit(dynamic_index_in_dim)/squeeze | solution.py:208
  33.9 0.8 collective-permute-start
  34.7 0.0 copy-done.13
  34.7 0.3 dynamic-slice_bitcast_fusion
  35.0 1.8 collective-permute-start.1
  36.8 6.1 %collective-permute-start.2 = (bf16[1024,704]{0,1:T(8,128)(2,1)S(1)}, bf16[1024,704]{0,1:T(8,128)(2,1)}, u32[]{:S(2)}, u32[]{:S(2)}) collective-permute-start(bf16[1024,704]{0,1:T(8,128)(2,1)S(1)} %get-tuple-element.13), channel_id=1, source_target_pairs={{0,1},{1,5},{2,0},{3,4},{4,3},{5,7},{6,2},{7,6},{8,9},{9,13},{10,8... | collective-permute-start | bytes 4325384 | tf_op jit(solution)/shard_map/ppermute | solution.py:209
  42.9 0.1 collective-permute-start.3
  43.0 0.0 collective-permute-done
  43.0 50.2 %collective-permute-start.4 = (bf16[1024,704]{0,1:T(8,128)(2,1)S(1)}, bf16[1024,704]{0,1:T(8,128)(2,1)}, u32[]{:S(2)}, u32[]{:S(2)}) collective-permute-start(bf16[1024,704]{0,1:T(8,128)(2,1)S(1)} %collective-permute-done), channel_id=1, source_target_pairs={{0,4},{4,0},{8,12},{12,8},{16,20},{20,16},{24,28},{28,24},{32,36},... | collective-permute-start | bytes 4325384 | tf_op jit(solution)/shard_map/ppermute | solution.py:211
  93.2 0.0 collective-permute-done.1
  93.2 34.8 %collective-permute-start.5 = (bf16[1024,704]{0,1:T(8,128)(2,1)}, bf16[1024,704]{0,1:T(8,128)(2,1)}, u32[]{:S(2)}, u32[]{:S(2)}) collective-permute-start(bf16[1024,704]{0,1:T(8,128)(2,1)} %collective-permute-done.1), channel_id=1, source_target_pairs={{0,4},{4,0},{8,12},{12,8},{16,20},{20,16},{24,28},{28,24},{32,36},... | collective-permute-start | bytes 4325384 | tf_op jit(solution)/shard_map/ppermute | solution.py:211
  128.1 0.0 collective-permute-done.2
  128.1 0.0 collective-permute-start.6
  128.1 3.4 %collective-permute-done.3 = bf16[1024,704]{0,1:T(8,128)(2,1)} collective-permute-done((bf16[1024,704]{0,1:T(8,128)(2,1)S(1)}, bf16[1024,704]{0,1:T(8,128)(2,1)}, u32[]{:S(2)}, u32[]{:S(2)}) %collective-permute-start.3) | collective-permute-done | bytes 1441824 | tf_op jit(solution)/shard_map/ppermute | solution.py:209
  131.4 1.6 collective-permute-start.7
  133.0 1.6 copy.18.refs_1_
  134.6 2.6 %copy.19.refs_2_ = bf16[1024,704]{1,0:T(8,128)(2,1)} copy(bf16[1024,704]{0,1:T(8,128)(2,1)} %collective-permute-done.1) | data formatting | bytes 2883584 | tf_op jit(solution)/shard_map/ppermute | solution.py:209
  137.2 2.6 %copy.20.refs_3_ = bf16[1024,704]{1,0:T(8,128)(2,1)} copy(bf16[1024,704]{0,1:T(8,128)(2,1)} %collective-permute-done.2) | data formatting | bytes 2883584 | tf_op jit(solution)/shard_map/ppermute | solution.py:209
  139.8 2.6 %copy.21.refs_4_ = bf16[1024,704]{1,0:T(8,128)(2,1)} copy(bf16[1024,704]{0,1:T(8,128)(2,1)} %collective-permute-done.3) | data formatting | bytes 2883584 | tf_op jit(solution)/shard_map/ppermute | solution.py:209
  142.4 0.0 collective-permute-done.4
  142.4 2.6 %copy.22.refs_5_ = bf16[1024,704]{1,0:T(8,128)(2,1)} copy(bf16[1024,704]{0,1:T(8,128)(2,1)} %collective-permute-done.4) | data formatting | bytes 2883584 | tf_op jit(solution)/shard_map/ppermute | solution.py:211
  144.9 0.0 collective-permute-done.5
  144.9 2.6 %copy.23.refs_6_ = bf16[1024,704]{1,0:T(8,128)(2,1)} copy(bf16[1024,704]{0,1:T(8,128)(2,1)} %collective-permute-done.5) | data formatting | bytes 2883584 | tf_op jit(solution)/shard_map/ppermute | solution.py:211
  147.5 0.0 collective-permute-done.6
  147.5 2.6 %copy.24.refs_7_ = bf16[1024,704]{1,0:T(8,128)(2,1)} copy(bf16[1024,704]{0,1:T(8,128)(2,1)} %collective-permute-done.6) | data formatting | bytes 2883584 | tf_op jit(solution)/shard_map/ppermute | solution.py:211
  150.1 0.0 collective-permute-done.7
  150.1 2.6 %copy.25.refs_8_ = bf16[1024,704]{1,0:T(8,128)(2,1)} copy(bf16[1024,704]{0,1:T(8,128)(2,1)} %collective-permute-done.7) | data formatting | bytes 2883584 | tf_op jit(solution)/shard_map/ppermute | solution.py:211
  152.7 0.0 all-to-all-done.refs_0_
  152.7 20.0 %expert.1 = bf16[64,2,8,512]{3,2,1,0:T(8,128)(2,1)} custom-call(bf16[128,8,1536]{2,1,0:T(8,128)(2,1)} %all-to-all-done.refs_0_, bf16[1024,704]{1,0:T(8,128)(2,1)} %copy.18.refs_1_, bf16[1024,704]{1,0:T(8,128)(2,1)} %copy.19.refs_2_, bf16[1024,704]{1,0:T(8,128)(2,1)} %copy.20.refs_3_, bf16[1024,704]{1,0:T(8,128)(2,1)} %copy.21.refs_4_, ...), custom_call_target="tpu_custom_call" | custom-call | tf_op jit(solution)/shard_map/expert/pallas_call | solution.py:156
  172.7 0.0 copy-start.7
  172.7 0.0 copy-start.9
  172.7 0.0 copy-start.11
  172.7 39.7 %all_to_all.10 = bf16[128,8,512]{2,1,0:T(8,128)(2,1)S(1)} all-to-all(bf16[128,8,512]{2,1,0:T(8,128)(2,1)} %bitcast.34), channel_id=1, replica_groups={{0,1,2,3,8,9,10,11,16,17,18,19,24,25,26,27,32,33,34,35,40,41,42,43,48,4..., dimensions={0} | all-to-all | bytes 2097152 | tf_op jit(solution)/shard_map/all_to_all | solution.py:229
  212.4 0.0 copy-done.7
  212.4 0.0 copy-done.9
  212.4 0.0 copy-done.11
  212.4 1.6 combine.1
Async XLA Ops:
  0.7 1.6 copy-start
  2.2 1.0 copy-start.1
  3.3 1.0 copy-start.2
  4.3 1.0 copy-start.3
  5.4 0.9 copy-start.4
  6.3 0.9 copy-start.5
  7.3 0.7 copy-start.6
  8.0 0.7 copy-start.8
  8.6 0.7 copy-start.10
  9.3 0.7 copy-start.12
  16.2 136.5 %all-to-all-start = ((bf16[128,8,1536]{2,1,0:T(8,128)(2,1)}), bf16[128,8,1536]{2,1,0:T(8,128)(2,1)}, u32[]{:S(2)}, u32[]{:S(2)}) async-start(bf16[128,8,1536]{2,1,0:T(8,128)(2,1)} %bitcast.35), calls=%async_computation | async-start | bytes 6291456 | tf_op jit(solution)/shard_map/all_to_all | solution.py:229
  31.7 3.0 %copy-start.13 = (bf16[2,1024,704]{1,2,0:T(8,128)(2,1)S(1)}, bf16[2,1024,704]{1,2,0:T(8,128)(2,1)}, u32[]{:S(2)}) copy-start(bf16[2,1024,704]{1,2,0:T(8,128)(2,1)} %param.24) | copy-start | bytes 8650756
  33.9 9.0 %collective-permute-start = (bf16[1024,704]{0,1:T(8,128)(2,1)S(1)}, bf16[1024,704]{0,1:T(8,128)(2,1)S(1)}, u32[]{:S(2)}, u32[]{:S(2)}) collective-permute-start(bf16[1024,704]{0,1:T(8,128)(2,1)S(1)} %get-tuple-element.14), channel_id=1, source_target_pairs={{0,0},{1,4},{2,1},{3,5},{4,2},{5,6},{6,3},{7,7},{8,8},{9,12},{10,9... | collective-permute-start | bytes 4325384 | tf_op jit(solution)/shard_map/ppermute | solution.py:209
  35.0 58.2 %collective-permute-start.1 = (bf16[1024,704]{0,1:T(8,128)(2,1)S(1)}, bf16[1024,704]{0,1:T(8,128)(2,1)}, u32[]{:S(2)}, u32[]{:S(2)}) collective-permute-start(bf16[1024,704]{0,1:T(8,128)(2,1)S(1)} %get-tuple-element.12), channel_id=1, source_target_pairs={{0,0},{1,4},{2,1},{3,5},{4,2},{5,6},{6,3},{7,7},{8,8},{9,12},{10,9... | collective-permute-start | bytes 4325384 | tf_op jit(solution)/shard_map/ppermute | solution.py:209
  36.8 91.3 %collective-permute-start.2 = (bf16[1024,704]{0,1:T(8,128)(2,1)S(1)}, bf16[1024,704]{0,1:T(8,128)(2,1)}, u32[]{:S(2)}, u32[]{:S(2)}) collective-permute-start(bf16[1024,704]{0,1:T(8,128)(2,1)S(1)} %get-tuple-element.13), channel_id=1, source_target_pairs={{0,1},{1,5},{2,0},{3,4},{4,3},{5,7},{6,2},{7,6},{8,9},{9,13},{10,8... | collective-permute-start | bytes 4325384 | tf_op jit(solution)/shard_map/ppermute | solution.py:209
  42.9 88.6 %collective-permute-start.3 = (bf16[1024,704]{0,1:T(8,128)(2,1)S(1)}, bf16[1024,704]{0,1:T(8,128)(2,1)}, u32[]{:S(2)}, u32[]{:S(2)}) collective-permute-start(bf16[1024,704]{0,1:T(8,128)(2,1)S(1)} %get-tuple-element.11), channel_id=1, source_target_pairs={{0,1},{1,5},{2,0},{3,4},{4,3},{5,7},{6,2},{7,6},{8,9},{9,13},{10,8... | collective-permute-start | bytes 4325384 | tf_op jit(solution)/shard_map/ppermute | solution.py:209
  43.0 99.4 %collective-permute-start.4 = (bf16[1024,704]{0,1:T(8,128)(2,1)S(1)}, bf16[1024,704]{0,1:T(8,128)(2,1)}, u32[]{:S(2)}, u32[]{:S(2)}) collective-permute-start(bf16[1024,704]{0,1:T(8,128)(2,1)S(1)} %collective-permute-done), channel_id=1, source_target_pairs={{0,4},{4,0},{8,12},{12,8},{16,20},{20,16},{24,28},{28,24},{32,36},... | collective-permute-start | bytes 4325384 | tf_op jit(solution)/shard_map/ppermute | solution.py:211
  93.2 51.7 %collective-permute-start.5 = (bf16[1024,704]{0,1:T(8,128)(2,1)}, bf16[1024,704]{0,1:T(8,128)(2,1)}, u32[]{:S(2)}, u32[]{:S(2)}) collective-permute-start(bf16[1024,704]{0,1:T(8,128)(2,1)} %collective-permute-done.1), channel_id=1, source_target_pairs={{0,4},{4,0},{8,12},{12,8},{16,20},{20,16},{24,28},{28,24},{32,36},... | collective-permute-start | bytes 4325384 | tf_op jit(solution)/shard_map/ppermute | solution.py:211
  128.1 19.5 %collective-permute-start.6 = (bf16[1024,704]{0,1:T(8,128)(2,1)}, bf16[1024,704]{0,1:T(8,128)(2,1)}, u32[]{:S(2)}, u32[]{:S(2)}) collective-permute-start(bf16[1024,704]{0,1:T(8,128)(2,1)} %collective-permute-done.2), channel_id=1, source_target_pairs={{0,4},{4,0},{8,12},{12,8},{16,20},{20,16},{24,28},{28,24},{32,36},... | collective-permute-start | bytes 4325384 | tf_op jit(solution)/shard_map/ppermute | solution.py:211
  131.4 18.7 %collective-permute-start.7 = (bf16[1024,704]{0,1:T(8,128)(2,1)}, bf16[1024,704]{0,1:T(8,128)(2,1)}, u32[]{:S(2)}, u32[]{:S(2)}) collective-permute-start(bf16[1024,704]{0,1:T(8,128)(2,1)} %collective-permute-done.3), channel_id=1, source_target_pairs={{0,4},{4,0},{8,12},{12,8},{16,20},{20,16},{24,28},{28,24},{32,36},... | collective-permute-start | bytes 4325384 | tf_op jit(solution)/shard_map/ppermute | solution.py:211
  172.7 39.7 %copy-start.7 = (f32[1024]{0:T(1024)S(1)}, f32[1024]{0:T(1024)}, u32[]{:S(2)}) copy-start(f32[1024]{0:T(1024)} %param.22) | copy-start | bytes 12292
  172.7 39.7 %copy-start.9 = (s32[1,1,256]{2,1,0:T(1,128)S(1)}, s32[1,1,256]{2,1,0:T(1,128)}, u32[]{:S(2)}) copy-start(s32[1,1,256]{2,1,0:T(1,128)} %param.19) | copy-start | bytes 3076
  172.7 39.7 %copy-start.11 = (s32[1,1,256]{2,1,0:T(1,128)S(1)}, s32[1,1,256]{2,1,0:T(1,128)}, u32[]{:S(2)}) copy-start(s32[1,1,256]{2,1,0:T(1,128)} %param.20) | copy-start | bytes 3076

commit v2 on v1

--- a/solution.py
+++ b/solution.py
@@ -28,9 +28,9 @@
 
 
 def prepare_kernel(
-    length_ref, ids_ref, slots_ref, gate_ref, gain_ref, enc_hbm, base_hbm, keys_hbm, query_hbm, mult_hbm, wv_hbm,
+    length_ref, ids_hbm, slots_hbm, gate_hbm, gain_hbm, enc_hbm, base_hbm, keys_hbm, query_hbm, mult_hbm, wv_hbm,
     placed_ref, layer_ref, scale_ref,
-    enc_ref, base_ref, keys_ref, query_ref, mult_ref, wv_ref, value_ref, sems,
+    ids_ref, slots_ref, gate_ref, gain_ref, enc_ref, base_ref, keys_ref, query_ref, mult_ref, wv_ref, value_ref, sems,
 ):
     enc_len, width = enc_ref.shape
     dec_len = query_ref.shape[0]
@@ -40,6 +40,7 @@
             (
                 (keys_hbm, keys_ref), (query_hbm, query_ref), (mult_hbm, mult_ref),
                 (wv_hbm, wv_ref), (enc_hbm, enc_ref), (base_hbm, base_ref),
+                (ids_hbm, ids_ref), (slots_hbm, slots_ref), (gate_hbm, gate_ref), (gain_hbm, gain_ref),
             )
         )
     ]
@@ -61,6 +62,8 @@
         attn = (expo * (1.0 / jnp.sum(expo, axis=0, keepdims=True))).astype(BF16)
         value_ref[:, lanes] = mm(attn, mults).astype(BF16)
     copies[3].wait()
+    for copy in copies[6:]:
+        copy.wait()
     layer_mult = mm_nt(value_ref[...], wv_ref[...])
     layer_ref[...] = layer_mult
     scaled_mult = (column_of(gate_ref[...]) * layer_mult).astype(BF16)
@@ -84,86 +87,89 @@
 
 def prepare(length, ids, slots, gate, gain, enc, base, keys, query, mult, wv, n_rows):
     enc_len, width = enc.shape
-    any_spec = pl.BlockSpec(memory_space=pl.ANY)
     vmem = pl.BlockSpec(memory_space=pltpu.VMEM)
+    taken = (ids, slots, gate, gain, enc, base, keys, query, mult, wv)
     return pl.pallas_call(
         prepare_kernel,
-        in_specs=[pl.BlockSpec(memory_space=pltpu.SMEM)] + [vmem] * 4 + [any_spec] * 6,
+        in_specs=[pl.BlockSpec(memory_space=pltpu.SMEM)] + [pl.BlockSpec(memory_space=pltpu.HBM)] * len(taken),
         out_specs=[vmem] * 3,
         out_shape=[
             jax.ShapeDtypeStruct((n_rows, 3 * width // 2), BF16),
             jax.ShapeDtypeStruct((enc_len, width), F32),
             jax.ShapeDtypeStruct((enc_len, 128), F32),
         ],
-        scratch_shapes=[pltpu.VMEM(a.shape, BF16) for a in (enc, base, keys, query, mult, wv)]
-        + [pltpu.VMEM((enc_len, width), BF16), pltpu.SemaphoreType.DMA((6,))],
-        compiler_params=pltpu.CompilerParams(vmem_limit_bytes=48 << 20),
+        scratch_shapes=[pltpu.VMEM(a.shape, a.dtype) for a in taken]
+        + [pltpu.VMEM((enc_len, width), BF16), pltpu.SemaphoreType.DMA((len(taken),))],
+        compiler_params=pltpu.CompilerParams(vmem_limit_bytes=62 << 20),
         name="prepare",
-    )(length, ids, slots, gate, gain, enc, base, keys, query, mult, wv)
+    )(length, *taken)
 
 
 def expert_kernel(rows_ref, *refs, n_parts):
-    weights_hbm = refs[: 2 * n_parts]
-    out_ref = refs[2 * n_parts]
-    weights = refs[2 * n_parts + 1 : 4 * n_parts + 1]
-    in_ref, base_ref, mult_ref, acc_ref, sems = refs[4 * n_parts + 1 :]
+    bundles_hbm = refs[:n_parts]
+    out_ref, in_ref, mult_ref, w_in_ref, w_out_ref, act_ref, sems = refs[n_parts:]
+    part_len = bundles_hbm[0].shape[0] // 2
     copies = [
-        pltpu.make_async_copy(weights_hbm[i], weights[i], sems.at[i]) for i in range(2 * n_parts)
+        pltpu.make_async_copy(
+            bundles_hbm[part].at[pl.ds(which * part_len, part_len)],
+            ref.at[pl.ds(part * part_len, part_len)],
+            sems.at[2 * part + which],
+        )
+        for part in range(n_parts)
+        for which, ref in enumerate((w_in_ref, w_out_ref))
     ]
     for copy in copies:
         copy.start()
     n_tiles, _, lanes = rows_ref.shape
     half = lanes // 3
+    n_rows = n_tiles * 4
     upper_rows = lax.broadcasted_iota(jnp.int32, (n_tiles // 2, 8, half), 1) < 4
-    for i, ref in enumerate((in_ref, base_ref, mult_ref)):
+    for i, ref in enumerate((in_ref.at[:n_rows], in_ref.at[n_rows:], mult_ref)):
         block = rows_ref[:, :, i * half : (i + 1) * half].astype(F32).reshape(n_tiles // 2, 2, 8, half)
         even, odd = block[:, 0], block[:, 1]
         low = jnp.where(upper_rows, even, pltpu.roll(odd, 4, 1))
         high = jnp.where(upper_rows, pltpu.roll(even, 4, 1), odd)
-        ref[:, :half] = low.reshape(n_tiles * 4, half).astype(BF16)
-        ref[:, half:] = high.reshape(n_tiles * 4, half).astype(BF16)
-    n_rows = n_tiles * 4
-    block = n_rows // 2
-    for part in range(n_parts):
-        copies[2 * part].wait()
-        copies[2 * part + 1].wait()
-        part_in, part_out = weights[2 * part], weights[2 * part + 1]
-        for at in range(0, n_rows, block):
-            rows = slice(at, at + block)
-            pre_act = mm(in_ref[rows, :], part_in[...])
-            base_act = mm(base_ref[rows, :], part_in[...])
-            hidden_mult = mm(mult_ref[rows, :], part_out[...])
-            upper_part = jnp.maximum(jnp.maximum(pre_act, base_act), 0.0)
-            lower_part = jnp.maximum(-jnp.minimum(pre_act, base_act), 0.0)
-            ratio = upper_part / (upper_part + lower_part + jnp.where(upper_part > 0.0, 0.0, 1.0))
-            term = mm_nt((ratio * hidden_mult).astype(BF16), part_in[...])
-            if part == 0:
-                acc_ref[rows, :] = term
-            else:
-                acc_ref[rows, :] += term
-    low = acc_ref[:, :half].reshape(n_tiles // 2, 8, half)
-    high = acc_ref[:, half:].reshape(n_tiles // 2, 8, half)
-    even = jnp.where(upper_rows, low, pltpu.roll(high, 4, 1)).astype(BF16)
-    odd = jnp.where(upper_rows, pltpu.roll(low, 4, 1), high).astype(BF16)
-    out_ref[:, 0] = even
-    out_ref[:, 1] = odd
+        ref[:, :half] = low.reshape(n_rows, half).astype(BF16)
+        ref[:, half:] = high.reshape(n_rows, half).astype(BF16)
+    hidden = n_parts * part_len
+    block = 256
+    waited = 0
+    for at in range(0, hidden, block):
+        cols = slice(at, at + block)
+        while waited < 2 * n_parts and waited // 2 * part_len < at + block:
+            copies[waited].wait()
+            waited += 1
+        both = mm_nt(in_ref[...], w_in_ref[cols, :])
+        pre_act, base_act = both[:n_rows], both[n_rows:]
+        hidden_mult = mm_nt(mult_ref[...], w_out_ref[cols, :])
+        upper_part = jnp.maximum(jnp.maximum(pre_act, base_act), 0.0)
+        lower_part = jnp.maximum(-jnp.minimum(pre_act, base_act), 0.0)
+        ratio = upper_part / (upper_part + lower_part + jnp.where(upper_part > 0.0, 0.0, 1.0))
+        act_ref[:, cols] = (ratio * hidden_mult).astype(BF16)
+    low = mm(act_ref[...], w_in_ref[:, :half]).reshape(n_tiles // 2, 8, half)
+    high = mm(act_ref[...], w_in_ref[:, half:]).reshape(n_tiles // 2, 8, half)
+    out_ref[:, 0] = jnp.where(upper_rows, low, pltpu.roll(high, 4, 1)).astype(BF16)
+    out_ref[:, 1] = jnp.where(upper_rows, pltpu.roll(low, 4, 1), high).astype(BF16)
 
 
 def expert_terms(rows, parts):
     n_tiles, _, lanes = rows.shape
     half = lanes // 3
-    flat = [w for pair in parts for w in pair]
+    n_rows, width = n_tiles * 4, 2 * half
+    hidden = len(parts) * (parts[0].shape[0] // 2)
     out = pl.pallas_call(
         lambda *refs: expert_kernel(*refs, n_parts=len(parts)),
-        in_specs=[pl.BlockSpec(memory_space=pltpu.VMEM)] + [pl.BlockSpec(memory_space=pl.ANY)] * len(flat),
+        in_specs=[pl.BlockSpec(memory_space=pltpu.VMEM)] + [pl.BlockSpec(memory_space=pltpu.HBM)] * len(parts),
         out_specs=pl.BlockSpec(memory_space=pltpu.VMEM),
         out_shape=jax.ShapeDtypeStruct((n_tiles // 2, 2, 8, half), BF16),
-        scratch_shapes=[pltpu.VMEM(w.shape, BF16) for w in flat]
-        + [pltpu.VMEM((n_tiles * 4, 2 * half), BF16)] * 3
-        + [pltpu.VMEM((n_tiles * 4, 2 * half), F32), pltpu.SemaphoreType.DMA((len(flat),))],
-        compiler_params=pltpu.CompilerParams(vmem_limit_bytes=56 << 20),
+        scratch_shapes=[
+            pltpu.VMEM((2 * n_rows, width), BF16), pltpu.VMEM((n_rows, width), BF16),
+            pltpu.VMEM((hidden, width), BF16), pltpu.VMEM((hidden, width), BF16),
+            pltpu.VMEM((n_rows, hidden), BF16), pltpu.SemaphoreType.DMA((2 * len(parts),)),
+        ],
+        compiler_params=pltpu.CompilerParams(vmem_limit_bytes=62 << 20),
         name="expert",
-    )(rows, *flat)
+    )(rows, *parts)
     return out.reshape(n_tiles, 8, half)
 
 
@@ -193,24 +199,37 @@
 
 def exchange_weights(w_in, w_out_t, n_expert_devices):
     axes = ("expert", "dp")
-    dp_at = lax.axis_index("dp")
-    pieces = []
-    for step in range(2):
-        pairs = []
-        for chip in range(n_expert_devices // 2):
-            for core in range(2):
-                for part in range(4):
-                    own = (part // 2 + step) % 2
-                    to_dp, to_core = 2 * core + own, part % 2
-                    pairs.append(((chip * 2 + core) * 4 + part, (chip * 2 + to_core) * 4 + to_dp))
-        own = (dp_at // 2 + step) % 2
-        for weights in (w_in, w_out_t):
-            sent = lax.dynamic_index_in_dim(weights, own, 0, keepdims=False)
-            pieces.append(lax.ppermute(sent, axes, pairs))
+    first_round, second_round = [], []
+    for chip in range(n_expert_devices // 2):
+        for core in range(2):
+            for at in range(4):
+                home = at // 2
+                here = (chip * 2 + core) * 4 + at
+                if core == home:
+                    first_to, first_core = at ^ 1, 1 - home
+                    second_to, second_core = at ^ 1, home
+                else:
+                    first_to, first_core = 3 - at, core
+                    second_to, second_core = 3 - at, 1 - core
+                first_round.append((here, (chip * 2 + first_core) * 4 + first_to))
+                second_round.append((here, (chip * 2 + second_core) * 4 + second_to))
+    at = lax.axis_index("dp")
+    is_home = (at // 2) == (lax.axis_index("expert") % 2)
+    first = jnp.where(is_home, 1 - at % 2, at % 2)
+    w_in, w_out_t = jnp.swapaxes(w_in, 1, 2), jnp.swapaxes(w_out_t, 1, 2)
+
+    def bundle(own):
+        return jnp.concatenate(
+            [lax.dynamic_index_in_dim(w, own, 0, keepdims=False) for w in (w_in, w_out_t)], axis=0
+        )
+
+    came = lax.ppermute(bundle(first), axes, first_round)
+    rest = bundle(1 - first)
+    kept = jnp.where(is_home, rest, came)
+    onward = jnp.where(is_home, came, rest)
     swap = [(i, i ^ 1) for i in range(n_expert_devices)]
-    swapped = [lax.ppermute(piece, "expert", swap) for piece in pieces]
-    both = pieces + swapped
-    return list(zip(both[0::2], both[1::2]))
+    last = lax.ppermute(onward, axes, second_round)
+    return [kept, lax.ppermute(kept, "expert", swap), last, lax.ppermute(last, "expert", swap)]
 
 
 def body(

time: 215 us -> 181 us (0.84)
  starting transfers between devices: 111 us -> 18.9 us
  waiting for transfers between devices: 3.38 us -> 78.6 us
  local copies, waits for them, and re-layouts: 31.5 us -> 6.06 us
  other arithmetic: 0 us -> 4.66 us
  blocking collectives: 39.7 us -> 44.2 us
    ppermute x8 -> x4, starting transfers between devices: 95.4 us -> 3.95 us  [the longest x1 1.88 us: exchange_weights(): lax.ppermute(kept, 'expert', swap)]
    ppermute x8 -> x4, waiting for transfers between devices: 3.38 us -> 78.6 us  [the longest x1 49.6 us: exchange_weights(): last = lax.ppermute(onward, axes, second_round)]
    ppermute x8 -> x0, local copies, waits for them, and re-layouts: 19.7 us -> none  [the longest x4 10.3 us: exchange_weights(): swapped = [lax.ppermute(piece, 'expert', swap) for piece in pieces]]
    unnamed x28 -> x14, local copies, waits for them, and re-layouts: 9.35 us -> 1.54 us
    all_to_all x1, blocking collectives: 39.7 us -> 44.2 us  [exchange(): lax.all_to_all(rows, axes, split_axis=0, concat_axis=0, axis_index_groups...]
    select_n x0 -> x1, other arithmetic: none -> 2.85 us  [exchange_weights(): onward = jnp.where(is_home, came, rest)]
    squeeze x2 -> x1, local copies, waits for them, and re-layouts: 2.51 us -> 4.53 us  [bundle(): lax.dynamic_index_in_dim(w, own, 0, keepdims=False)]
  transfers between devices with their start and end apart: 9 -> 5, of which waited for: 1 -> 3; matrix products, arithmetic and copies ran while one was open for 10% -> 2% of each run, Pallas kernels for 0% -> 4%
where the time goes in v2:
time: 181 us
  waiting for transfers between devices  78.6 us (43%)
  blocking collectives  44.2 us (24%)
  Pallas kernels  28 us (15%)
  starting transfers between devices  18.9 us (10%)
  local copies, waits for them, and re-layouts  6.06 us (3%)
  other arithmetic  4.66 us (3%)
    ppermute x1, waiting for transfers between devices, exchange_weights(): last = lax.ppermute(onward, axes, second_round)  49.6 us
    all_to_all x1, blocking collectives, exchange(): lax.all_to_all(rows, axes, split_axis=0, concat_axis=0, axis_index_groups...  44.2 us
    ppermute x1, waiting for transfers between devices, exchange_weights(): came = lax.ppermute(bundle(first), axes, first_round)  23.8 us
    pallas_call x1, Pallas kernels, expert_terms(): pl.pallas_call(lambda *refs: expert_kernel(*refs, n_parts=len(parts)), in...  19.2 us
    all_to_all x1, starting transfers between devices, exchange(): lax.all_to_all(rows, axes, split_axis=0, concat_axis=0, axis_index_groups...  15 us
    pallas_call x1, Pallas kernels, prepare(): pl.pallas_call(prepare_kernel, in_specs=[pl.BlockSpec(memory_space=pltpu....  7.15 us
    ppermute x1, waiting for transfers between devices, exchange_weights(): lax.ppermute(last, 'expert', swap)  5.25 us
    squeeze x1, local copies, waits for them, and re-layouts, bundle(): lax.dynamic_index_in_dim(w, own, 0, keepdims=False)  4.53 us
  transfers between devices with their start and end apart: 5, of which 3 were waited for; matrix products, arithmetic and copies ran while one was open for 2% of the time, Pallas kernels for 4%

profile of v2, /device:TPU:32, one launch (start us, length us, event | category | flops | bytes accessed | tf_op | source)
XLA Modules:
  0.0 181.1 jit_solution(2895354248919966345)
XLA Ops:
  0.0 4.5 %dynamic-slice_bitcast_fusion.2 = (bf16[704,1024]{1,0:T(8,128)(2,1)S(1)}, bf16[704,1024]{1,0:T(8,128)(2,1)S(1)}, bf16[704,1024]{1,0:T(8,128)(2,1)S(1)}, bf16[704,1024]{1,0:T(8,128)(2,1)}) fusion(bf16[2,1024,704]{1,2,0:T(8,128)(2,1)} %param.24, s32[]{:T(128)S(6)} %select_n.46, s32[]{:T(128)S(6)} %select_n.47, bf16[2,1024,704]{1,2,0:T(8,128)(2,1)} %param.23), kind=kLoop, calls=%fused_computation.6 | loop fusion | bytes 11534344 | tf_op jit(solution)/shard_map/jit(dynamic_index_in_dim)/squeeze | solution.py:223
  4.5 1.8 pad_maximum_fusion.1
  6.3 1.0 collective-permute-start
  8.0 7.2 %prepare.1 = (bf16[1024,1536]{1,0:T(8,128)(2,1)}, f32[256,1024]{1,0:T(8,128)}, f32[256,128]{1,0:T(8,128)}) custom-call(s32[1,1]{1,0:T(1,128)S(6)} %copy.14.length_ref, s32[1,256]{1,0:T(1,128)} %bitcast.32, s32[1,256]{1,0:T(1,128)} %bitcast.34, f32[1,256]{1,0:T(1,128)} %bitcast.43, f32[1,1024]{1,0:T(1,128)} %bitcast.30, bf16[256,1024]{1,0:T(8,128)(2,1)} %bitcast.38, ...), custom_call_target="tpu_custom_call" | custom-call | tf_op jit(solution)/shard_map/prepare/pallas_call | solution.py:92
  15.2 0.0 copy-start.6
  15.2 15.0 %all-to-all-start = ((bf16[128,8,1536]{2,1,0:T(8,128)(2,1)}), bf16[128,8,1536]{2,1,0:T(8,128)(2,1)}, u32[]{:S(2)}, u32[]{:S(2)}) async-start(bf16[128,8,1536]{2,1,0:T(8,128)(2,1)} %bitcast.37), calls=%async_computation | async-start | bytes 6291456 | tf_op jit(solution)/shard_map/all_to_all | solution.py:248
  30.2 23.8 %collective-permute-done = bf16[1408,1024]{1,0:T(8,128)(2,1)} collective-permute-done((bf16[1408,1024]{1,0:T(8,128)(2,1)}, bf16[1408,1024]{1,0:T(8,128)(2,1)}, u32[]{:S(2)}, u32[]{:S(2)}) %collective-permute-start) | collective-permute-done | bytes 2883616 | tf_op jit(solution)/shard_map/ppermute | solution.py:226
  53.9 0.0 copy-done.6
  53.9 2.8 %broadcast_select_fusion = (bf16[1408,1024]{1,0:T(8,128)(2,1)S(1)}, bf16[1408,1024]{1,0:T(8,128)(2,1)S(1)}) fusion(bf16[1408,1024]{1,0:T(8,128)(2,1)} %collective-permute-done, pred[]{:T(512)S(6)} %eq.7, bf16[704,1024]{1,0:T(8,128)(2,1)S(1)} %get-tuple-element.15, bf16[704,1024]{1,0:T(8,128)(2,1)S(1)} %copy-done.6), kind=kLoop, calls=%fused_computation.2 | loop fusion | flops 8650752 | bytes 11534337 | tf_op jit(solution)/shard_map/jit(_where)/select_n | solution.py:229
  56.8 0.0 copy-start.5
  56.8 0.1 collective-permute-start.2
  56.9 1.5 copy-done.5
  58.4 0.0 copy-start
  58.4 0.0 copy-start.1
  58.4 0.0 copy-start.2
  58.4 0.0 copy-start.3
  58.4 0.0 copy-start.4
  58.4 1.9 %collective-permute-start.1 = (bf16[1408,1024]{1,0:T(8,128)(2,1)S(1)}, bf16[1408,1024]{1,0:T(8,128)(2,1)}, u32[]{:S(2)}, u32[]{:S(2)}) collective-permute-start(bf16[1408,1024]{1,0:T(8,128)(2,1)S(1)} %get-tuple-element.12.refs_1_), channel_id=1, source_target_pairs={{0,4},{4,0},{8,12},{12,8},{16,20},{20,16},{24,28},{28,24},{32,36},... | collective-permute-start | bytes 8650760 | tf_op jit(solution)/shard_map/ppermute | solution.py:232
  60.3 49.6 %collective-permute-done.2.refs_3_ = bf16[1408,1024]{1,0:T(8,128)(2,1)} collective-permute-done((bf16[1408,1024]{1,0:T(8,128)(2,1)S(1)}, bf16[1408,1024]{1,0:T(8,128)(2,1)}, u32[]{:S(2)}, u32[]{:S(2)}) %collective-permute-start.2) | collective-permute-done | bytes 2883616 | tf_op jit(solution)/shard_map/ppermute | solution.py:231
  109.9 1.0 collective-permute-start.3
  110.8 0.0 collective-permute-done.1.refs_2_
  110.8 0.0 all-to-all-done.refs_0_
  110.8 5.2 %collective-permute-done.3.refs_4_ = bf16[1408,1024]{1,0:T(8,128)(2,1)} collective-permute-done((bf16[1408,1024]{1,0:T(8,128)(2,1)}, bf16[1408,1024]{1,0:T(8,128)(2,1)}, u32[]{:S(2)}, u32[]{:S(2)}) %collective-permute-start.3) | collective-permute-done | bytes 2883616 | tf_op jit(solution)/shard_map/ppermute | solution.py:232
  116.1 19.2 %expert.1 = bf16[64,2,8,512]{3,2,1,0:T(8,128)(2,1)} custom-call(bf16[128,8,1536]{2,1,0:T(8,128)(2,1)} %all-to-all-done.refs_0_, bf16[1408,1024]{1,0:T(8,128)(2,1)} %copy-done.5, bf16[1408,1024]{1,0:T(8,128)(2,1)} %collective-permute-done.1.refs_2_, bf16[1408,1024]{1,0:T(8,128)(2,1)} %collective-permute-done.2.refs_3_, ...), custom_call_target="tpu_custom_call" | custom-call | tf_op jit(solution)/shard_map/expert/pallas_call | solution.py:160
  135.3 44.2 %all_to_all.10 = bf16[128,8,512]{2,1,0:T(8,128)(2,1)S(1)} all-to-all(bf16[128,8,512]{2,1,0:T(8,128)(2,1)} %bitcast.36), channel_id=1, replica_groups={{0,1,2,3,8,9,10,11,16,17,18,19,24,25,26,27,32,33,34,35,40,41,42,43,48,4..., dimensions={0} | all-to-all | bytes 2097152 | tf_op jit(solution)/shard_map/all_to_all | solution.py:248
  179.5 0.0 copy-done
  179.5 0.0 copy-done.1
  179.5 0.0 copy-done.2
  179.5 0.0 copy-done.3
  179.5 0.0 copy-done.4
  179.5 1.6 combine.1
Async XLA Ops:
  6.3 47.6 %collective-permute-start = (bf16[1408,1024]{1,0:T(8,128)(2,1)}, bf16[1408,1024]{1,0:T(8,128)(2,1)}, u32[]{:S(2)}, u32[]{:S(2)}) collective-permute-start(bf16[1408,1024]{1,0:T(8,128)(2,1)} %pad_maximum_fusion.1), channel_id=1, source_target_pairs={{0,5},{1,4},{2,1},{3,0},{4,7},{5,6},{6,3},{7,2},{8,13},{9,12},{10,... | collective-permute-start | bytes 8650760 | tf_op jit(solution)/shard_map/ppermute | solution.py:226
  15.2 38.8 %copy-start.6 = (bf16[704,1024]{1,0:T(8,128)(2,1)S(1)}, bf16[704,1024]{1,0:T(8,128)(2,1)}, u32[]{:S(2)}) copy-start(bf16[704,1024]{1,0:T(8,128)(2,1)} %get-tuple-element.18) | copy-start | bytes 4325380
  15.2 95.7 %all-to-all-start = ((bf16[128,8,1536]{2,1,0:T(8,128)(2,1)}), bf16[128,8,1536]{2,1,0:T(8,128)(2,1)}, u32[]{:S(2)}, u32[]{:S(2)}) async-start(bf16[128,8,1536]{2,1,0:T(8,128)(2,1)} %bitcast.37), calls=%async_computation | async-start | bytes 6291456 | tf_op jit(solution)/shard_map/all_to_all | solution.py:248
  56.8 1.6 copy-start.5
  56.8 53.1 %collective-permute-start.2 = (bf16[1408,1024]{1,0:T(8,128)(2,1)S(1)}, bf16[1408,1024]{1,0:T(8,128)(2,1)}, u32[]{:S(2)}, u32[]{:S(2)}) collective-permute-start(bf16[1408,1024]{1,0:T(8,128)(2,1)S(1)} %get-tuple-element.11), channel_id=1, source_target_pairs={{0,1},{1,0},{2,5},{3,4},{4,3},{5,2},{6,7},{7,6},{8,9},{9,8},{10,13... | collective-permute-start | bytes 8650760 | tf_op jit(solution)/shard_map/ppermute | solution.py:231
  58.4 121.1 %copy-start = (f32[256,1024]{1,0:T(8,128)S(1)}, f32[256,1024]{1,0:T(8,128)}, u32[]{:S(2)}) copy-start(f32[256,1024]{1,0:T(8,128)} %get-tuple-element.9.layer_ref) | copy-start | bytes 3145732
  58.4 121.1 %copy-start.1 = (f32[256,128]{1,0:T(8,128)S(1)}, f32[256,128]{1,0:T(8,128)}, u32[]{:S(2)}) copy-start(f32[256,128]{1,0:T(8,128)} %get-tuple-element.8.scale_ref) | copy-start | bytes 393220
  58.4 121.1 %copy-start.2 = (f32[1024]{0:T(1024)S(1)}, f32[1024]{0:T(1024)}, u32[]{:S(2)}) copy-start(f32[1024]{0:T(1024)} %param.22) | copy-start | bytes 12292
  58.4 121.1 %copy-start.3 = (s32[1,1,256]{2,1,0:T(1,128)S(1)}, s32[1,1,256]{2,1,0:T(1,128)}, u32[]{:S(2)}) copy-start(s32[1,1,256]{2,1,0:T(1,128)} %param.19) | copy-start | bytes 3076
  58.4 121.1 %copy-start.4 = (s32[1,1,256]{2,1,0:T(1,128)S(1)}, s32[1,1,256]{2,1,0:T(1,128)}, u32[]{:S(2)}) copy-start(s32[1,1,256]{2,1,0:T(1,128)} %param.20) | copy-start | bytes 3076
  58.4 52.4 %collective-permute-start.1 = (bf16[1408,1024]{1,0:T(8,128)(2,1)S(1)}, bf16[1408,1024]{1,0:T(8,128)(2,1)}, u32[]{:S(2)}, u32[]{:S(2)}) collective-permute-start(bf16[1408,1024]{1,0:T(8,128)(2,1)S(1)} %get-tuple-element.12.refs_1_), channel_id=1, source_target_pairs={{0,4},{4,0},{8,12},{12,8},{16,20},{20,16},{24,28},{28,24},{32,36},... | collective-permute-start | bytes 8650760 | tf_op jit(solution)/shard_map/ppermute | solution.py:232
  109.9 6.2 %collective-permute-start.3 = (bf16[1408,1024]{1,0:T(8,128)(2,1)}, bf16[1408,1024]{1,0:T(8,128)(2,1)}, u32[]{:S(2)}, u32[]{:S(2)}) collective-permute-start(bf16[1408,1024]{1,0:T(8,128)(2,1)} %collective-permute-done.2.refs_3_), channel_id=1, source_target_pairs={{0,4},{4,0},{8,12},{12,8},{16,20},{20,16},{24,28},{28,24},{32,36},... | collective-permute-start | bytes 8650760 | tf_op jit(solution)/shard_map/ppermute | solution.py:232

commit v3 on v2

--- a/solution.py
+++ b/solution.py
@@ -105,26 +105,30 @@
     )(length, *taken)
 
 
-def expert_kernel(rows_ref, *refs, n_parts):
-    bundles_hbm = refs[:n_parts]
-    out_ref, in_ref, mult_ref, w_in_ref, w_out_ref, act_ref, sems = refs[n_parts:]
-    part_len = bundles_hbm[0].shape[0] // 2
-    copies = [
-        pltpu.make_async_copy(
-            bundles_hbm[part].at[pl.ds(which * part_len, part_len)],
-            ref.at[pl.ds(part * part_len, part_len)],
-            sems.at[2 * part + which],
-        )
-        for part in range(n_parts)
-        for which, ref in enumerate((w_in_ref, w_out_ref))
-    ]
-    for copy in copies:
-        copy.start()
+def expert_kernel(rows_hbm, *refs, n_parts):
+    weights_hbm = refs[: 2 * n_parts]
+    out_ref, rows_ref, in_ref, mult_ref, w_in_ref, w_out_ref, act_ref, sems = refs[2 * n_parts :]
     n_tiles, _, lanes = rows_ref.shape
     half = lanes // 3
     n_rows = n_tiles * 4
+    part_len = weights_hbm[0].shape[0]
+    copies = [
+        pltpu.make_async_copy(
+            weights_hbm[i], (w_in_ref, w_out_ref)[i % 2].at[pl.ds(i // 2 * part_len, part_len)], sems.at[i]
+        )
+        for i in range(2 * n_parts)
+    ]
+    row_copies = []
+    for i in range(3):
+        lanes_of = (slice(None), slice(None), pl.ds(i * half, half))
+        row_copies.append(
+            pltpu.make_async_copy(rows_hbm.at[lanes_of], rows_ref.at[lanes_of], sems.at[2 * n_parts + i])
+        )
+    for copy in [*row_copies[:2], copies[0], row_copies[2], *copies[1:]]:
+        copy.start()
     upper_rows = lax.broadcasted_iota(jnp.int32, (n_tiles // 2, 8, half), 1) < 4
     for i, ref in enumerate((in_ref.at[:n_rows], in_ref.at[n_rows:], mult_ref)):
+        row_copies[i].wait()
         block = rows_ref[:, :, i * half : (i + 1) * half].astype(F32).reshape(n_tiles // 2, 2, 8, half)
         even, odd = block[:, 0], block[:, 1]
         low = jnp.where(upper_rows, even, pltpu.roll(odd, 4, 1))
@@ -156,16 +160,17 @@
     n_tiles, _, lanes = rows.shape
     half = lanes // 3
     n_rows, width = n_tiles * 4, 2 * half
-    hidden = len(parts) * (parts[0].shape[0] // 2)
+    n_parts = len(parts) // 2
+    hidden = n_parts * parts[0].shape[0]
     out = pl.pallas_call(
-        lambda *refs: expert_kernel(*refs, n_parts=len(parts)),
-        in_specs=[pl.BlockSpec(memory_space=pltpu.VMEM)] + [pl.BlockSpec(memory_space=pltpu.HBM)] * len(parts),
+        lambda *refs: expert_kernel(*refs, n_parts=n_parts),
+        in_specs=[pl.BlockSpec(memory_space=pltpu.HBM)] * (1 + len(parts)),
         out_specs=pl.BlockSpec(memory_space=pltpu.VMEM),
         out_shape=jax.ShapeDtypeStruct((n_tiles // 2, 2, 8, half), BF16),
         scratch_shapes=[
-            pltpu.VMEM((2 * n_rows, width), BF16), pltpu.VMEM((n_rows, width), BF16),
+            pltpu.VMEM(rows.shape, BF16), pltpu.VMEM((2 * n_rows, width), BF16), pltpu.VMEM((n_rows, width), BF16),
             pltpu.VMEM((hidden, width), BF16), pltpu.VMEM((hidden, width), BF16),
-            pltpu.VMEM((n_rows, hidden), BF16), pltpu.SemaphoreType.DMA((2 * len(parts),)),
+            pltpu.VMEM((n_rows, hidden), BF16), pltpu.SemaphoreType.DMA((len(parts) + 3,)),
         ],
         compiler_params=pltpu.CompilerParams(vmem_limit_bytes=62 << 20),
         name="expert",
@@ -197,7 +202,7 @@
     )(ids, slots, gain, scale, layer_mult, back)
 
 
-def exchange_weights(w_in, w_out_t, n_expert_devices):
+def exchange_weights(w_in, w_out_t, rows, n_expert_devices):
     axes = ("expert", "dp")
     first_round, second_round = [], []
     for chip in range(n_expert_devices // 2):
@@ -218,18 +223,23 @@
     first = jnp.where(is_home, 1 - at % 2, at % 2)
     w_in, w_out_t = jnp.swapaxes(w_in, 1, 2), jnp.swapaxes(w_out_t, 1, 2)
 
-    def bundle(own):
-        return jnp.concatenate(
-            [lax.dynamic_index_in_dim(w, own, 0, keepdims=False) for w in (w_in, w_out_t)], axis=0
-        )
-
-    came = lax.ppermute(bundle(first), axes, first_round)
-    rest = bundle(1 - first)
-    kept = jnp.where(is_home, rest, came)
-    onward = jnp.where(is_home, came, rest)
     swap = [(i, i ^ 1) for i in range(n_expert_devices)]
-    last = lax.ppermute(onward, axes, second_round)
-    return [kept, lax.ppermute(kept, "expert", swap), last, lax.ppermute(last, "expert", swap)]
+    kept, last = [], []
+    for weights in (w_in, w_out_t):
+        came = lax.ppermute(lax.dynamic_index_in_dim(weights, first, 0, keepdims=False), axes, first_round)
+        came, late = lax.optimization_barrier((came, weights))
+        rest = lax.dynamic_index_in_dim(late, 1 - first, 0, keepdims=False)
+        kept.append(jnp.where(is_home, rest, came))
+        last.append(lax.ppermute(jnp.where(is_home, came, rest), axes, second_round))
+    kept = lax.optimization_barrier(kept)
+    other = []
+    for i, piece in enumerate(kept + last):
+        if other:
+            other[-1], piece = lax.optimization_barrier((other[-1], piece))
+        if i == 3:
+            rows, piece = lax.optimization_barrier((rows, piece))
+        other.append(lax.ppermute(piece, "expert", swap))
+    return rows, kept + last + other
 
 
 def body(
@@ -247,13 +257,13 @@
     def exchange(rows):
         return lax.all_to_all(rows, axes, split_axis=0, concat_axis=0, axis_index_groups=groups, tiled=True)
 
-    parts = exchange_weights(w_in, w_out_t, n_expert_devices)
     ids, slots, gain = expert_ids[0], slot_ids[0], norm_gain[None, :]
     placed, layer_mult, scale = prepare(
         doc_lengths, ids, slots, gate_prob[0], gain, enc_state[0, 0], baseline[0, 0], enc_keys[0, 0],
         dec_queries[0, 0], out_mult[0, 0], w_value, n_experts * 8,
     )
     came = exchange(placed.reshape(n_experts, 8, 3 * width // 2))
+    came, parts = exchange_weights(w_in, w_out_t, came, n_expert_devices)
     slot_mult = expert_terms(came, parts)
     back = exchange(slot_mult)
     result = combine(ids, slots, gain, scale, layer_mult, back.reshape(n_experts * 8, width // 2))

time: 181 us -> 177 us (0.978)
  waiting for transfers between devices: 78.6 us -> 74.2 us
  starting transfers between devices: 18.9 us -> 21.6 us
    ppermute x4 -> x8, waiting for transfers between devices: 78.6 us -> 74.2 us  [the longest x2 48.4 us: exchange_weights(): lax.ppermute(jnp.where(is_home, came, rest), axes, second_round)]
    ppermute x4 -> x8, starting transfers between devices: 3.95 us -> 7.22 us  [the longest x4 4.91 us: exchange_weights(): other.append(lax.ppermute(piece, 'expert', swap))]
    select_n x1 -> x2, other arithmetic: 2.85 us -> 3.78 us  [exchange_weights(): jnp.where(is_home, came, rest)]
    squeeze x1 -> x2, local copies, waits for them, and re-layouts: 4.53 us -> 3.94 us  [exchange_weights(): lax.dynamic_index_in_dim(weights, first, 0, keepdims=False)]
  transfers between devices with their start and end apart: 5 -> 9, of which waited for: 3 -> 5; matrix products, arithmetic and copies ran while one was open for 2% -> 3% of each run, Pallas kernels for 4% -> 4%
where the time goes in v3:
time: 177 us
  waiting for transfers between devices  74.2 us (42%)
  blocking collectives  44 us (25%)
  Pallas kernels  27.1 us (15%)
  starting transfers between devices  21.6 us (12%)
  local copies, waits for them, and re-layouts  5.61 us (3%)
  other arithmetic  3.78 us (2%)
    ppermute x2, waiting for transfers between devices, exchange_weights(): lax.ppermute(jnp.where(is_home, came, rest), axes, second_round)  48.4 us
    all_to_all x1, blocking collectives, exchange(): lax.all_to_all(rows, axes, split_axis=0, concat_axis=0, axis_index_groups...  44 us
    ppermute x2, waiting for transfers between devices, exchange_weights(): lax.ppermute(lax.dynamic_index_in_dim(weights, first, 0, keepdims=False),...  19.6 us
    pallas_call x1, Pallas kernels, expert_terms(): pl.pallas_call(lambda *refs: expert_kernel(*refs, n_parts=n_parts), in_sp...  18.3 us
    all_to_all x1, starting transfers between devices, exchange(): lax.all_to_all(rows, axes, split_axis=0, concat_axis=0, axis_index_groups...  14.4 us
    pallas_call x1, Pallas kernels, prepare(): pl.pallas_call(prepare_kernel, in_specs=[pl.BlockSpec(memory_space=pltpu....  7.16 us
    ppermute x4, waiting for transfers between devices, exchange_weights(): other.append(lax.ppermute(piece, 'expert', swap))  6.13 us
    ppermute x4, starting transfers between devices, exchange_weights(): other.append(lax.ppermute(piece, 'expert', swap))  4.91 us
  transfers between devices with their start and end apart: 9, of which 5 were waited for; matrix products, arithmetic and copies ran while one was open for 3% of the time, Pallas kernels for 4%

profile of v3, /device:TPU:32, one launch (start us, length us, event | category | flops | bytes accessed | tf_op | source)
XLA Modules:
  0.0 177.1 jit_solution(10659271095692582316)
XLA Ops:
  0.0 0.0 copy-start.8
  0.0 2.8 %dynamic-slice_bitcast_fusion.1 = bf16[704,1024]{1,0:T(8,128)(2,1)} fusion(bf16[2,1024,704]{1,2,0:T(8,128)(2,1)} %param.23, s32[]{:T(128)S(6)} %select_n.54), kind=kLoop, calls=%fused_computation.5 | loop fusion | bytes 2883588 | tf_op jit(solution)/shard_map/jit(dynamic_index_in_dim)/squeeze | solution.py:229
  2.8 1.0 collective-permute-start
  3.8 0.0 copy-done.8
  3.8 1.2 dynamic-slice_bitcast_fusion
  5.0 1.3 collective-permute-start.1
  6.9 7.2 %prepare.1 = (bf16[1024,1536]{1,0:T(8,128)(2,1)}, f32[256,1024]{1,0:T(8,128)}, f32[256,128]{1,0:T(8,128)}) custom-call(s32[1,1]{1,0:T(1,128)S(6)} %copy.14.length_ref, s32[1,256]{1,0:T(1,128)} %bitcast.32, s32[1,256]{1,0:T(1,128)} %bitcast.34, f32[1,256]{1,0:T(1,128)} %bitcast.45, f32[1,1024]{1,0:T(1,128)} %bitcast.30, bf16[256,1024]{1,0:T(8,128)(2,1)} %bitcast.40, ...), custom_call_target="tpu_custom_call" | custom-call | tf_op jit(solution)/shard_map/prepare/pallas_call | solution.py:92
  14.1 0.0 copy-start.7
  14.1 14.4 %all-to-all-start = ((bf16[128,8,1536]{2,1,0:T(8,128)(2,1)}), bf16[128,8,1536]{2,1,0:T(8,128)(2,1)}, u32[]{:S(2)}, u32[]{:S(2)}) async-start(bf16[128,8,1536]{2,1,0:T(8,128)(2,1)} %bitcast.37), calls=%async_computation | async-start | bytes 6291456 | tf_op jit(solution)/shard_map/all_to_all | solution.py:258
  28.5 0.0 collective-permute-done
  28.5 19.6 %collective-permute-done.1 = bf16[704,1024]{1,0:T(8,128)(2,1)} collective-permute-done((bf16[704,1024]{1,0:T(8,128)(2,1)}, bf16[704,1024]{1,0:T(8,128)(2,1)}, u32[]{:S(2)}, u32[]{:S(2)}) %collective-permute-start.1) | collective-permute-done | bytes 1441824 | tf_op jit(solution)/shard_map/ppermute | solution.py:229
  48.1 0.0 copy-done.7
  48.1 0.0 copy-start.9
  48.1 1.7 bitcast_select_fusion.2
  49.9 0.5 copy-done.9
  50.4 0.0 copy-start.5
  50.4 2.1 %bitcast_select_fusion = (bf16[704,1024]{1,0:T(8,128)(2,1)S(1)}, bf16[704,1024]{1,0:T(8,128)(2,1)S(1)}) fusion(bf16[704,1024]{1,0:T(8,128)(2,1)} %collective-permute-done.1, pred[]{:T(512)S(6)} %eq.7, bf16[2,704,1024]{2,1,0:T(8,128)(2,1)S(1)} %bitcast.39, s32[]{:T(128)S(6)} %select_n.55), kind=kLoop, calls=%fused_computation | loop fusion | flops 1441792 | bytes 5767173 | tf_op jit(solution)/shard_map/jit(_where)/select_n | solution.py:233
  52.5 0.0 copy-start.6
  52.5 0.0 copy-done.5
  52.5 3.5 %collective-permute-start.2 = (bf16[704,1024]{1,0:T(8,128)(2,1)S(1)}, bf16[704,1024]{1,0:T(8,128)(2,1)S(1)}, u32[]{:S(2)}, u32[]{:S(2)}) collective-permute-start(bf16[704,1024]{1,0:T(8,128)(2,1)S(1)} %get-tuple-element.29.refs_1_), channel_id=1, source_target_pairs={{0,4},{4,0},{8,12},{12,8},{16,20},{20,16},{24,28},{28,24},{32,36},... | collective-permute-start | bytes 4325384 | tf_op jit(solution)/shard_map/ppermute | solution.py:241
  56.0 0.0 collective-permute-start.4
  56.0 2.8 %collective-permute-done.2.refs_5_ = bf16[704,1024]{1,0:T(8,128)(2,1)S(1)} collective-permute-done((bf16[704,1024]{1,0:T(8,128)(2,1)S(1)}, bf16[704,1024]{1,0:T(8,128)(2,1)S(1)}, u32[]{:S(2)}, u32[]{:S(2)}) %collective-permute-start.2) | collective-permute-done | bytes 1441824 | tf_op jit(solution)/shard_map/ppermute | solution.py:241
  58.9 0.0 copy-done.6
  58.9 0.0 copy-start.10
  58.9 1.0 collective-permute-start.3
  59.9 0.0 collective-permute-start.6
  59.9 29.3 %collective-permute-done.4.refs_3_ = bf16[704,1024]{1,0:T(8,128)(2,1)S(1)} collective-permute-done((bf16[704,1024]{1,0:T(8,128)(2,1)S(1)}, bf16[704,1024]{1,0:T(8,128)(2,1)S(1)}, u32[]{:S(2)}, u32[]{:S(2)}) %collective-permute-start.4) | collective-permute-done | bytes 1441824 | tf_op jit(solution)/shard_map/ppermute | solution.py:233
  89.1 0.0 copy-start.11
  89.1 0.0 collective-permute-done.3.refs_6_
  89.1 0.0 copy-start.12
  89.1 0.3 collective-permute-start.5
  89.4 19.2 %collective-permute-done.6.refs_4_ = bf16[704,1024]{1,0:T(8,128)(2,1)S(1)} collective-permute-done((bf16[704,1024]{1,0:T(8,128)(2,1)S(1)}, bf16[704,1024]{1,0:T(8,128)(2,1)S(1)}, u32[]{:S(2)}, u32[]{:S(2)}) %collective-permute-start.6) | collective-permute-done | bytes 1441824 | tf_op jit(solution)/shard_map/ppermute | solution.py:233
  108.6 0.0 copy-done.11
  108.6 0.0 copy-done.12
  108.6 0.0 copy-start.13
  108.6 0.0 collective-permute-done.5.refs_7_
  108.6 0.0 all-to-all-done.refs_0_
  108.7 1.1 copy-done.13
  109.7 0.1 collective-permute-start.7
  109.8 3.3 %collective-permute-done.7.refs_8_ = bf16[704,1024]{1,0:T(8,128)(2,1)} collective-permute-done((bf16[704,1024]{1,0:T(8,128)(2,1)S(1)}, bf16[704,1024]{1,0:T(8,128)(2,1)}, u32[]{:S(2)}, u32[]{:S(2)}) %collective-permute-start.7) | collective-permute-done | bytes 1441824 | tf_op jit(solution)/shard_map/ppermute | solution.py:241
  113.1 0.0 copy-done.10
  113.1 18.3 %expert.1 = bf16[64,2,8,512]{3,2,1,0:T(8,128)(2,1)} custom-call(bf16[128,8,1536]{2,1,0:T(8,128)(2,1)} %all-to-all-done.refs_0_, bf16[704,1024]{1,0:T(8,128)(2,1)} %copy-done.5, bf16[704,1024]{1,0:T(8,128)(2,1)} %copy-done.6, bf16[704,1024]{1,0:T(8,128)(2,1)} %copy-done.11, bf16[704,1024]{1,0:T(8,128)(2,1)} %copy-done.13, bf16[704,1024]{1,0:T(8,128)(2,1)} %copy-done.10, ...), custom_call_target="tpu_custom_call" | custom-call | tf_op jit(solution)/shard_map/expert/pallas_call | solution.py:165
  131.4 0.0 copy-start
  131.4 0.0 copy-start.1
  131.4 0.0 copy-start.2
  131.4 0.0 copy-start.3
  131.4 0.0 copy-start.4
  131.5 44.0 %all_to_all.10 = bf16[128,8,512]{2,1,0:T(8,128)(2,1)S(1)} all-to-all(bf16[128,8,512]{2,1,0:T(8,128)(2,1)} %bitcast.36), channel_id=1, replica_groups={{0,1,2,3,8,9,10,11,16,17,18,19,24,25,26,27,32,33,34,35,40,41,42,43,48,4..., dimensions={0} | all-to-all | bytes 2097152 | tf_op jit(solution)/shard_map/all_to_all | solution.py:258
  175.4 0.0 copy-done
  175.4 0.0 copy-done.1
  175.4 0.0 copy-done.2
  175.4 0.0 copy-done.3
  175.4 0.0 copy-done.4
  175.4 1.6 combine.1
Async XLA Ops:
  0.0 3.8 %copy-start.8 = (bf16[2,1024,704]{1,2,0:T(8,128)(2,1)S(1)}, bf16[2,1024,704]{1,2,0:T(8,128)(2,1)}, u32[]{:S(2)}) copy-start(bf16[2,1024,704]{1,2,0:T(8,128)(2,1)} %param.24) | copy-start | bytes 8650756
  2.8 25.8 %collective-permute-start = (bf16[704,1024]{1,0:T(8,128)(2,1)}, bf16[704,1024]{1,0:T(8,128)(2,1)}, u32[]{:S(2)}, u32[]{:S(2)}) collective-permute-start(bf16[704,1024]{1,0:T(8,128)(2,1)} %dynamic-slice_bitcast_fusion.1), channel_id=1, source_target_pairs={{0,5},{1,4},{2,1},{3,0},{4,7},{5,6},{6,3},{7,2},{8,13},{9,12},{10,... | collective-permute-start | bytes 4325384 | tf_op jit(solution)/shard_map/ppermute | solution.py:229
  5.0 43.2 %collective-permute-start.1 = (bf16[704,1024]{1,0:T(8,128)(2,1)}, bf16[704,1024]{1,0:T(8,128)(2,1)}, u32[]{:S(2)}, u32[]{:S(2)}) collective-permute-start(bf16[704,1024]{1,0:T(8,128)(2,1)} %dynamic-slice_bitcast_fusion), channel_id=1, source_target_pairs={{0,5},{1,4},{2,1},{3,0},{4,7},{5,6},{6,3},{7,2},{8,13},{9,12},{10,... | collective-permute-start | bytes 4325384 | tf_op jit(solution)/shard_map/ppermute | solution.py:229
  14.1 34.1 %copy-start.7 = (bf16[2,1024,704]{1,2,0:T(8,128)(2,1)S(1)}, bf16[2,1024,704]{1,2,0:T(8,128)(2,1)}, u32[]{:S(2)}) copy-start(bf16[2,1024,704]{1,2,0:T(8,128)(2,1)} %param.23) | copy-start | bytes 8650756
  14.1 94.6 %all-to-all-start = ((bf16[128,8,1536]{2,1,0:T(8,128)(2,1)}), bf16[128,8,1536]{2,1,0:T(8,128)(2,1)}, u32[]{:S(2)}, u32[]{:S(2)}) async-start(bf16[128,8,1536]{2,1,0:T(8,128)(2,1)} %bitcast.37), calls=%async_computation | async-start | bytes 6291456 | tf_op jit(solution)/shard_map/all_to_all | solution.py:258
  48.1 2.2 %copy-start.9 = (bf16[2,1024,704]{1,2,0:T(8,128)(2,1)S(1)}, bf16[2,1024,704]{1,2,0:T(8,128)(2,1)}, u32[]{:S(2)}) copy-start(bf16[2,1024,704]{1,2,0:T(8,128)(2,1)} %param.24) | copy-start | bytes 8650756
  50.4 2.1 %copy-start.5 = (bf16[704,1024]{1,0:T(8,128)(2,1)}, bf16[704,1024]{1,0:T(8,128)(2,1)S(1)}, u32[]{:S(2)}) copy-start(bf16[704,1024]{1,0:T(8,128)(2,1)S(1)} %get-tuple-element.29.refs_1_) | copy-start | bytes 4325380
  52.5 6.4 %copy-start.6 = (bf16[704,1024]{1,0:T(8,128)(2,1)}, bf16[704,1024]{1,0:T(8,128)(2,1)S(1)}, u32[]{:S(2)}) copy-start(bf16[704,1024]{1,0:T(8,128)(2,1)S(1)} %get-tuple-element.31.refs_2_) | copy-start | bytes 4325380
  52.5 6.4 %collective-permute-start.2 = (bf16[704,1024]{1,0:T(8,128)(2,1)S(1)}, bf16[704,1024]{1,0:T(8,128)(2,1)S(1)}, u32[]{:S(2)}, u32[]{:S(2)}) collective-permute-start(bf16[704,1024]{1,0:T(8,128)(2,1)S(1)} %get-tuple-element.29.refs_1_), channel_id=1, source_target_pairs={{0,4},{4,0},{8,12},{12,8},{16,20},{20,16},{24,28},{28,24},{32,36},... | collective-permute-start | bytes 4325384 | tf_op jit(solution)/shard_map/ppermute | solution.py:241
  56.0 33.1 %collective-permute-start.4 = (bf16[704,1024]{1,0:T(8,128)(2,1)S(1)}, bf16[704,1024]{1,0:T(8,128)(2,1)S(1)}, u32[]{:S(2)}, u32[]{:S(2)}) collective-permute-start(bf16[704,1024]{1,0:T(8,128)(2,1)S(1)} %get-tuple-element.41), channel_id=1, source_target_pairs={{0,1},{1,0},{2,5},{3,4},{4,3},{5,2},{6,7},{7,6},{8,9},{9,8},{10,13... | collective-permute-start | bytes 4325384 | tf_op jit(solution)/shard_map/ppermute | solution.py:233
  58.9 54.2 %copy-start.10 = (bf16[704,1024]{1,0:T(8,128)(2,1)}, bf16[704,1024]{1,0:T(8,128)(2,1)S(1)}, u32[]{:S(2)}) copy-start(bf16[704,1024]{1,0:T(8,128)(2,1)S(1)} %collective-permute-done.2.refs_5_) | copy-start | bytes 4325380
  58.9 30.3 %collective-permute-start.3 = (bf16[704,1024]{1,0:T(8,128)(2,1)S(1)}, bf16[704,1024]{1,0:T(8,128)(2,1)S(1)}, u32[]{:S(2)}, u32[]{:S(2)}) collective-permute-start(bf16[704,1024]{1,0:T(8,128)(2,1)S(1)} %get-tuple-element.31.refs_2_), channel_id=1, source_target_pairs={{0,4},{4,0},{8,12},{12,8},{16,20},{20,16},{24,28},{28,24},{32,36},... | collective-permute-start | bytes 4325384 | tf_op jit(solution)/shard_map/ppermute | solution.py:241
  59.9 48.8 %collective-permute-start.6 = (bf16[704,1024]{1,0:T(8,128)(2,1)S(1)}, bf16[704,1024]{1,0:T(8,128)(2,1)S(1)}, u32[]{:S(2)}, u32[]{:S(2)}) collective-permute-start(bf16[704,1024]{1,0:T(8,128)(2,1)S(1)} %get-tuple-element.39), channel_id=1, source_target_pairs={{0,1},{1,0},{2,5},{3,4},{4,3},{5,2},{6,7},{7,6},{8,9},{9,8},{10,13... | collective-permute-start | bytes 4325384 | tf_op jit(solution)/shard_map/ppermute | solution.py:233
  89.1 19.5 %copy-start.11 = (bf16[704,1024]{1,0:T(8,128)(2,1)}, bf16[704,1024]{1,0:T(8,128)(2,1)S(1)}, u32[]{:S(2)}) copy-start(bf16[704,1024]{1,0:T(8,128)(2,1)S(1)} %collective-permute-done.4.refs_3_) | copy-start | bytes 4325380
  89.1 19.5 %copy-start.12 = (bf16[704,1024]{1,0:T(8,128)(2,1)}, bf16[704,1024]{1,0:T(8,128)(2,1)S(1)}, u32[]{:S(2)}) copy-start(bf16[704,1024]{1,0:T(8,128)(2,1)S(1)} %collective-permute-done.3.refs_6_) | copy-start | bytes 4325380
  89.1 19.5 %collective-permute-start.5 = (bf16[704,1024]{1,0:T(8,128)(2,1)S(1)}, bf16[704,1024]{1,0:T(8,128)(2,1)}, u32[]{:S(2)}, u32[]{:S(2)}) collective-permute-start(bf16[704,1024]{1,0:T(8,128)(2,1)S(1)} %collective-permute-done.4.refs_3_), channel_id=1, source_target_pairs={{0,4},{4,0},{8,12},{12,8},{16,20},{20,16},{24,28},{28,24},{32,36},... | collective-permute-start | bytes 4325384 | tf_op jit(solution)/shard_map/ppermute | solution.py:241
  108.6 1.1 copy-start.13
  109.7 3.4 %collective-permute-start.7 = (bf16[704,1024]{1,0:T(8,128)(2,1)S(1)}, bf16[704,1024]{1,0:T(8,128)(2,1)}, u32[]{:S(2)}, u32[]{:S(2)}) collective-permute-start(bf16[704,1024]{1,0:T(8,128)(2,1)S(1)} %collective-permute-done.6.refs_4_), channel_id=1, source_target_pairs={{0,4},{4,0},{8,12},{12,8},{16,20},{20,16},{24,28},{28,24},{32,36},... | collective-permute-start | bytes 4325384 | tf_op jit(solution)/shard_map/ppermute | solution.py:241
  131.4 44.0 %copy-start = (f32[256,1024]{1,0:T(8,128)S(1)}, f32[256,1024]{1,0:T(8,128)}, u32[]{:S(2)}) copy-start(f32[256,1024]{1,0:T(8,128)} %get-tuple-element.23.layer_ref) | copy-start | bytes 3145732
  131.4 44.0 %copy-start.1 = (f32[256,128]{1,0:T(8,128)S(1)}, f32[256,128]{1,0:T(8,128)}, u32[]{:S(2)}) copy-start(f32[256,128]{1,0:T(8,128)} %get-tuple-element.22.scale_ref) | copy-start | bytes 393220
  131.4 44.0 %copy-start.2 = (f32[1024]{0:T(1024)S(1)}, f32[1024]{0:T(1024)}, u32[]{:S(2)}) copy-start(f32[1024]{0:T(1024)} %param.22) | copy-start | bytes 12292
  131.4 44.0 %copy-start.3 = (s32[1,1,256]{2,1,0:T(1,128)S(1)}, s32[1,1,256]{2,1,0:T(1,128)}, u32[]{:S(2)}) copy-start(s32[1,1,256]{2,1,0:T(1,128)} %param.19) | copy-start | bytes 3076
  131.4 44.0 %copy-start.4 = (s32[1,1,256]{2,1,0:T(1,128)S(1)}, s32[1,1,256]{2,1,0:T(1,128)}, u32[]{:S(2)}) copy-start(s32[1,1,256]{2,1,0:T(1,128)} %param.20) | copy-start | bytes 3076

commit v4 on v3

--- a/solution.py
+++ b/solution.py
@@ -105,25 +105,37 @@
     )(length, *taken)
 
 
-def expert_kernel(rows_hbm, *refs, n_parts):
-    weights_hbm = refs[: 2 * n_parts]
-    out_ref, rows_ref, in_ref, mult_ref, w_in_ref, w_out_ref, act_ref, sems = refs[2 * n_parts :]
+def rescale(pre_act, base_act):
+    upper_part = jnp.maximum(jnp.maximum(pre_act, base_act), 0.0)
+    lower_part = jnp.maximum(-jnp.minimum(pre_act, base_act), 0.0)
+    return upper_part / (upper_part + lower_part + jnp.where(upper_part > 0.0, 0.0, 1.0))
+
+
+def hidden_blocks(length, block=256):
+    return [slice(at, min(at + block, length)) for at in range(0, length, block)]
+
+
+def first_kernel(
+    rows_hbm, kept_in, kept_in2, kept_out, kept_out2, last_in, last_in2,
+    partial_ref, ratio_ref, mult_ref, rows_ref, in_ref, w_in_ref, w_out_ref, act_ref, sems,
+):
     n_tiles, _, lanes = rows_ref.shape
     half = lanes // 3
     n_rows = n_tiles * 4
-    part_len = weights_hbm[0].shape[0]
+    part_len = kept_in.shape[0]
+    hidden = 2 * part_len
+
+    def part(src, dst, i, sem):
+        return pltpu.make_async_copy(src, dst.at[pl.ds(i * part_len, part_len)], sems.at[sem])
+
     copies = [
-        pltpu.make_async_copy(
-            weights_hbm[i], (w_in_ref, w_out_ref)[i % 2].at[pl.ds(i // 2 * part_len, part_len)], sems.at[i]
-        )
-        for i in range(2 * n_parts)
+        part(kept_in, w_in_ref, 0, 0), part(kept_out, w_out_ref, 0, 1), part(kept_in2, w_in_ref, 1, 2),
+        part(kept_out2, w_out_ref, 1, 3), part(last_in, w_in_ref, 2, 4), part(last_in2, w_in_ref, 3, 5),
     ]
     row_copies = []
     for i in range(3):
         lanes_of = (slice(None), slice(None), pl.ds(i * half, half))
-        row_copies.append(
-            pltpu.make_async_copy(rows_hbm.at[lanes_of], rows_ref.at[lanes_of], sems.at[2 * n_parts + i])
-        )
+        row_copies.append(pltpu.make_async_copy(rows_hbm.at[lanes_of], rows_ref.at[lanes_of], sems.at[6 + i]))
     for copy in [*row_copies[:2], copies[0], row_copies[2], *copies[1:]]:
         copy.start()
     upper_rows = lax.broadcasted_iota(jnp.int32, (n_tiles // 2, 8, half), 1) < 4
@@ -135,47 +147,96 @@
         high = jnp.where(upper_rows, pltpu.roll(even, 4, 1), odd)
         ref[:, :half] = low.reshape(n_rows, half).astype(BF16)
         ref[:, half:] = high.reshape(n_rows, half).astype(BF16)
-    hidden = n_parts * part_len
-    block = 256
-    waited = 0
-    for at in range(0, hidden, block):
-        cols = slice(at, at + block)
-        while waited < 2 * n_parts and waited // 2 * part_len < at + block:
-            copies[waited].wait()
-            waited += 1
+    for copy in copies[:2]:
+        copy.wait()
+    for i, cols in enumerate(hidden_blocks(hidden)):
+        if i == part_len // 256:
+            for copy in copies[2:4]:
+                copy.wait()
         both = mm_nt(in_ref[...], w_in_ref[cols, :])
-        pre_act, base_act = both[:n_rows], both[n_rows:]
         hidden_mult = mm_nt(mult_ref[...], w_out_ref[cols, :])
-        upper_part = jnp.maximum(jnp.maximum(pre_act, base_act), 0.0)
-        lower_part = jnp.maximum(-jnp.minimum(pre_act, base_act), 0.0)
-        ratio = upper_part / (upper_part + lower_part + jnp.where(upper_part > 0.0, 0.0, 1.0))
-        act_ref[:, cols] = (ratio * hidden_mult).astype(BF16)
-    low = mm(act_ref[...], w_in_ref[:, :half]).reshape(n_tiles // 2, 8, half)
-    high = mm(act_ref[...], w_in_ref[:, half:]).reshape(n_tiles // 2, 8, half)
+        act_ref[:, cols] = (rescale(both[:n_rows], both[n_rows:]) * hidden_mult).astype(BF16)
+    for copy in copies[4:]:
+        copy.wait()
+    for cols in hidden_blocks(hidden):
+        both = mm_nt(in_ref[...], w_in_ref[slice(hidden + cols.start, hidden + cols.stop), :])
+        ratio_ref[:, cols] = rescale(both[:n_rows], both[n_rows:])
+    partial_ref[...] = mm(act_ref[...], w_in_ref[:hidden, :])
+
+
+def last_kernel(
+    mult_ref, partial_hbm, ratio_hbm, last_in, last_in2, last_out, last_out2,
+    out_ref, partial_ref, ratio_ref, w_in_ref, w_out_ref, act_ref, sems,
+):
+    n_rows, width = mult_ref.shape
+    half = width // 2
+    n_tiles = n_rows // 4
+    part_len = last_in.shape[0]
+    hidden = 2 * part_len
+
+    def part(src, dst, i, sem):
+        return pltpu.make_async_copy(src, dst.at[pl.ds(i * part_len, part_len)], sems.at[sem])
+
+    copies = [
+        part(last_out, w_out_ref, 0, 0), pltpu.make_async_copy(ratio_hbm, ratio_ref, sems.at[1]),
+        part(last_out2, w_out_ref, 1, 2), part(last_in, w_in_ref, 0, 3), part(last_in2, w_in_ref, 1, 4),
+        pltpu.make_async_copy(partial_hbm, partial_ref, sems.at[5]),
+    ]
+    for copy in copies:
+        copy.start()
+    for copy in copies[:2]:
+        copy.wait()
+    for i, cols in enumerate(hidden_blocks(hidden)):
+        if i == part_len // 256:
+            copies[2].wait()
+        act_ref[:, cols] = (ratio_ref[:, cols] * mm_nt(mult_ref[...], w_out_ref[cols, :])).astype(BF16)
+    for copy in copies[3:]:
+        copy.wait()
+    upper_rows = lax.broadcasted_iota(jnp.int32, (n_tiles // 2, 8, half), 1) < 4
+    low = (partial_ref[:, :half] + mm(act_ref[...], w_in_ref[:, :half])).reshape(n_tiles // 2, 8, half)
+    high = (partial_ref[:, half:] + mm(act_ref[...], w_in_ref[:, half:])).reshape(n_tiles // 2, 8, half)
     out_ref[:, 0] = jnp.where(upper_rows, low, pltpu.roll(high, 4, 1)).astype(BF16)
     out_ref[:, 1] = jnp.where(upper_rows, pltpu.roll(low, 4, 1), high).astype(BF16)
 
 
-def expert_terms(rows, parts):
+def expert_first(rows, weights):
     n_tiles, _, lanes = rows.shape
-    half = lanes // 3
-    n_rows, width = n_tiles * 4, 2 * half
-    n_parts = len(parts) // 2
-    hidden = n_parts * parts[0].shape[0]
-    out = pl.pallas_call(
-        lambda *refs: expert_kernel(*refs, n_parts=n_parts),
-        in_specs=[pl.BlockSpec(memory_space=pltpu.HBM)] * (1 + len(parts)),
-        out_specs=pl.BlockSpec(memory_space=pltpu.VMEM),
-        out_shape=jax.ShapeDtypeStruct((n_tiles // 2, 2, 8, half), BF16),
+    n_rows, width = n_tiles * 4, 2 * lanes // 3
+    hidden = 2 * weights[0].shape[0]
+    return pl.pallas_call(
+        first_kernel,
+        in_specs=[pl.BlockSpec(memory_space=pltpu.HBM)] * 7,
+        out_specs=[pl.BlockSpec(memory_space=pltpu.VMEM)] * 3,
+        out_shape=[
+            jax.ShapeDtypeStruct((n_rows, width), F32), jax.ShapeDtypeStruct((n_rows, hidden), F32),
+            jax.ShapeDtypeStruct((n_rows, width), BF16),
+        ],
         scratch_shapes=[
-            pltpu.VMEM(rows.shape, BF16), pltpu.VMEM((2 * n_rows, width), BF16), pltpu.VMEM((n_rows, width), BF16),
-            pltpu.VMEM((hidden, width), BF16), pltpu.VMEM((hidden, width), BF16),
-            pltpu.VMEM((n_rows, hidden), BF16), pltpu.SemaphoreType.DMA((len(parts) + 3,)),
+            pltpu.VMEM(rows.shape, BF16), pltpu.VMEM((2 * n_rows, width), BF16),
+            pltpu.VMEM((2 * hidden, width), BF16), pltpu.VMEM((hidden, width), BF16),
+            pltpu.VMEM((n_rows, hidden), BF16), pltpu.SemaphoreType.DMA((9,)),
         ],
         compiler_params=pltpu.CompilerParams(vmem_limit_bytes=62 << 20),
-        name="expert",
-    )(rows, *parts)
-    return out.reshape(n_tiles, 8, half)
+        name="expert_first",
+    )(rows, *weights)
+
+
+def expert_last(mult, partial, ratio, weights):
+    n_rows, width = mult.shape
+    hidden = ratio.shape[1]
+    return pl.pallas_call(
+        last_kernel,
+        in_specs=[pl.BlockSpec(memory_space=pltpu.VMEM)] + [pl.BlockSpec(memory_space=pltpu.HBM)] * 6,
+        out_specs=pl.BlockSpec(memory_space=pltpu.VMEM),
+        out_shape=jax.ShapeDtypeStruct((n_rows // 8, 2, 8, width // 2), BF16),
+        scratch_shapes=[
+            pltpu.VMEM((n_rows, width), F32), pltpu.VMEM((n_rows, hidden), F32),
+            pltpu.VMEM((hidden, width), BF16), pltpu.VMEM((hidden, width), BF16),
+            pltpu.VMEM((n_rows, hidden), BF16), pltpu.SemaphoreType.DMA((6,)),
+        ],
+        compiler_params=pltpu.CompilerParams(vmem_limit_bytes=62 << 20),
+        name="expert_last",
+    )(mult, partial, ratio, *weights)
 
 
 def combine_kernel(ids_ref, slots_ref, gain_ref, scale_ref, layer_ref, back_ref, out_ref):
@@ -202,7 +263,7 @@
     )(ids, slots, gain, scale, layer_mult, back)
 
 
-def exchange_weights(w_in, w_out_t, rows, n_expert_devices):
+def expert_layer(w_in, w_out_t, rows, n_expert_devices):
     axes = ("expert", "dp")
     first_round, second_round = [], []
     for chip in range(n_expert_devices // 2):
@@ -233,13 +294,13 @@
         last.append(lax.ppermute(jnp.where(is_home, came, rest), axes, second_round))
     kept = lax.optimization_barrier(kept)
     other = []
-    for i, piece in enumerate(kept + last):
+    for piece in [*kept, last[0]]:
         if other:
             other[-1], piece = lax.optimization_barrier((other[-1], piece))
-        if i == 3:
-            rows, piece = lax.optimization_barrier((rows, piece))
         other.append(lax.ppermute(piece, "expert", swap))
-    return rows, kept + last + other
+    partial, ratio, mult = expert_first(rows, [kept[0], other[0], kept[1], other[1], last[0], other[2]])
+    partial, final = lax.optimization_barrier((partial, last[1]))
+    return expert_last(mult, partial, ratio, [last[0], other[2], final, lax.ppermute(final, "expert", swap)])
 
 
 def body(
@@ -263,9 +324,8 @@
         dec_queries[0, 0], out_mult[0, 0], w_value, n_experts * 8,
     )
     came = exchange(placed.reshape(n_experts, 8, 3 * width // 2))
-    came, parts = exchange_weights(w_in, w_out_t, came, n_expert_devices)
-    slot_mult = expert_terms(came, parts)
-    back = exchange(slot_mult)
+    slot_mult = expert_layer(w_in, w_out_t, came, n_expert_devices)
+    back = exchange(slot_mult.reshape(n_experts, 8, width // 2))
     result = combine(ids, slots, gain, scale, layer_mult, back.reshape(n_experts * 8, width // 2))
     return result[None, None]
 

time: 177 us -> 173 us (0.977)
  waiting for transfers between devices: 74.2 us -> 67.7 us
  blocking collectives: 44 us -> 38.5 us
  Pallas kernels: 27.1 us -> 32.5 us
    ppermute x8, waiting for transfers between devices: 74.2 us -> 57.6 us  [the longest x2 29.5 us: expert_layer(): lax.ppermute(jnp.where(is_home, came, rest), axes, second_round)]
    all_to_all x1, waiting for transfers between devices: 0.01 us -> 10.2 us  [exchange(): lax.all_to_all(rows, axes, split_axis=0, concat_axis=0, axis_index_groups...]
    all_to_all x1, blocking collectives: 44 us -> 38.5 us  [exchange(): lax.all_to_all(rows, axes, split_axis=0, concat_axis=0, axis_index_groups...]
    pallas_call x1 -> x2, Pallas kernels: 18.3 us -> 23.7 us  [the longest x1 15.3 us: expert_first(): pl.pallas_call(first_kernel, in_specs=[pl.BlockSpec(memory_space=pltpu.HB...]
  transfers between devices with their start and end apart: 9 -> 9, of which waited for: 5 -> 6; matrix products, arithmetic and copies ran while one was open for 3% -> 4% of each run, Pallas kernels for 4% -> 13%
where the time goes in v4:
time: 173 us
  waiting for transfers between devices  67.7 us (39%)
  blocking collectives  38.5 us (22%)
  Pallas kernels  32.5 us (19%)
  starting transfers between devices  21.7 us (13%)
  local copies, waits for them, and re-layouts  6.33 us (4%)
  other arithmetic  4.97 us (3%)
    all_to_all x1, blocking collectives, exchange(): lax.all_to_all(rows, axes, split_axis=0, concat_axis=0, axis_index_groups...  38.5 us
    ppermute x2, waiting for transfers between devices, expert_layer(): lax.ppermute(jnp.where(is_home, came, rest), axes, second_round)  29.5 us
    ppermute x2, waiting for transfers between devices, expert_layer(): lax.ppermute(lax.dynamic_index_in_dim(weights, first, 0, keepdims=False),...  19.5 us
    pallas_call x1, Pallas kernels, expert_first(): pl.pallas_call(first_kernel, in_specs=[pl.BlockSpec(memory_space=pltpu.HB...  15.3 us
    all_to_all x1, starting transfers between devices, exchange(): lax.all_to_all(rows, axes, split_axis=0, concat_axis=0, axis_index_groups...  14.4 us
    all_to_all x1, waiting for transfers between devices, exchange(): lax.all_to_all(rows, axes, split_axis=0, concat_axis=0, axis_index_groups...  10.2 us
    pallas_call x1, Pallas kernels, expert_last(): pl.pallas_call(last_kernel, in_specs=[pl.BlockSpec(memory_space=pltpu.VME...  8.47 us
    pallas_call x1, Pallas kernels, prepare(): pl.pallas_call(prepare_kernel, in_specs=[pl.BlockSpec(memory_space=pltpu....  7.15 us
  transfers between devices with their start and end apart: 9, of which 6 were waited for; matrix products, arithmetic and copies ran while one was open for 4% of the time, Pallas kernels for 13%

profile of v4, /device:TPU:32, one launch (start us, length us, event | category | flops | bytes accessed | tf_op | source)
XLA Modules:
  0.0 172.6 jit_solution(6169624302102877670)
XLA Ops:
  0.0 0.0 copy-start.9
  0.0 2.8 %dynamic-slice_bitcast_fusion = bf16[704,1024]{1,0:T(8,128)(2,1)} fusion(bf16[2,1024,704]{1,2,0:T(8,128)(2,1)} %param.24, s32[]{:T(128)S(6)} %select_n.54), kind=kLoop, calls=%fused_computation.4 | loop fusion | bytes 2883588 | tf_op jit(solution)/shard_map/jit(dynamic_index_in_dim)/squeeze | solution.py:290
  2.8 1.0 collective-permute-start.1
  3.8 0.0 copy-done.9
  3.8 1.2 dynamic-slice_bitcast_fusion.1
  5.1 1.3 collective-permute-start
  7.0 7.2 %prepare.1 = (bf16[1024,1536]{1,0:T(8,128)(2,1)}, f32[256,1024]{1,0:T(8,128)}, f32[256,128]{1,0:T(8,128)}) custom-call(s32[1,1]{1,0:T(1,128)S(6)} %copy.14.length_ref, s32[1,256]{1,0:T(1,128)} %bitcast.32, s32[1,256]{1,0:T(1,128)} %bitcast.34, f32[1,256]{1,0:T(1,128)} %bitcast.45, f32[1,1024]{1,0:T(1,128)} %bitcast.30, bf16[256,1024]{1,0:T(8,128)(2,1)} %bitcast.40, ...), custom_call_target="tpu_custom_call" | custom-call | tf_op jit(solution)/shard_map/prepare/pallas_call | solution.py:92
  14.2 0.0 copy-start.8
  14.2 14.4 %all-to-all-start = ((bf16[128,8,1536]{2,1,0:T(8,128)(2,1)}), bf16[128,8,1536]{2,1,0:T(8,128)(2,1)}, u32[]{:S(2)}, u32[]{:S(2)}) async-start(bf16[128,8,1536]{2,1,0:T(8,128)(2,1)} %bitcast.37), calls=%async_computation | async-start | bytes 6291456 | tf_op jit(solution)/shard_map/all_to_all | solution.py:319
  28.6 0.0 collective-permute-done.1
  28.7 19.5 %collective-permute-done = bf16[704,1024]{1,0:T(8,128)(2,1)} collective-permute-done((bf16[704,1024]{1,0:T(8,128)(2,1)}, bf16[704,1024]{1,0:T(8,128)(2,1)}, u32[]{:S(2)}, u32[]{:S(2)}) %collective-permute-start) | collective-permute-done | bytes 1441824 | tf_op jit(solution)/shard_map/ppermute | solution.py:290
  48.2 0.0 copy-done.8
  48.2 0.0 copy-start.10
  48.2 2.9 %bitcast_select_fusion = (bf16[704,1024]{1,0:T(8,128)(2,1)}, bf16[704,1024]{1,0:T(8,128)(2,1)S(1)}) fusion(bf16[704,1024]{1,0:T(8,128)(2,1)} %collective-permute-done.1, pred[]{:T(512)S(6)} %eq.7, bf16[2,704,1024]{2,1,0:T(8,128)(2,1)S(1)} %bitcast.38, s32[]{:T(128)S(6)} %select_n.55), kind=kLoop, calls=%fused_computation | loop fusion | flops 1441792 | bytes 5767173 | tf_op jit(solution)/shard_map/jit(_where)/select_n | solution.py:294
  51.1 0.0 copy-done.10
  51.1 0.0 copy-start.6
  51.1 2.1 %bitcast_select_fusion.2 = (bf16[704,1024]{1,0:T(8,128)(2,1)S(1)}, bf16[704,1024]{1,0:T(8,128)(2,1)S(1)}) fusion(bf16[704,1024]{1,0:T(8,128)(2,1)} %collective-permute-done, pred[]{:T(512)S(6)} %eq.7, bf16[2,704,1024]{2,1,0:T(8,128)(2,1)S(1)} %bitcast.39, s32[]{:T(128)S(6)} %select_n.55), kind=kLoop, calls=%fused_computation.2 | loop fusion | flops 1441792 | bytes 5767173 | tf_op jit(solution)/shard_map/jit(_where)/select_n | solution.py:294
  53.2 0.0 copy-start.7
  53.2 3.5 %collective-permute-start.2 = (bf16[704,1024]{1,0:T(8,128)(2,1)S(1)}, bf16[704,1024]{1,0:T(8,128)(2,1)S(1)}, u32[]{:S(2)}, u32[]{:S(2)}) collective-permute-start(bf16[704,1024]{1,0:T(8,128)(2,1)S(1)} %get-tuple-element.30.kept_in), channel_id=1, source_target_pairs={{0,4},{4,0},{8,12},{12,8},{16,20},{20,16},{24,28},{28,24},{32,36},... | collective-permute-start | bytes 4325384 | tf_op jit(solution)/shard_map/ppermute | solution.py:300
  56.7 0.0 collective-permute-start.4
  56.7 2.8 %collective-permute-done.2.kept_in2 = bf16[704,1024]{1,0:T(8,128)(2,1)S(1)} collective-permute-done((bf16[704,1024]{1,0:T(8,128)(2,1)S(1)}, bf16[704,1024]{1,0:T(8,128)(2,1)S(1)}, u32[]{:S(2)}, u32[]{:S(2)}) %collective-permute-start.2) | collective-permute-done | bytes 1441824 | tf_op jit(solution)/shard_map/ppermute | solution.py:300
  59.6 0.0 copy-done.6
  59.6 0.0 copy-start.12
  59.6 1.0 collective-permute-start.3
  60.6 29.5 %collective-permute-done.4.last_in = bf16[704,1024]{1,0:T(8,128)(2,1)S(1)} collective-permute-done((bf16[704,1024]{1,0:T(8,128)(2,1)S(1)}, bf16[704,1024]{1,0:T(8,128)(2,1)S(1)}, u32[]{:S(2)}, u32[]{:S(2)}) %collective-permute-start.4) | collective-permute-done | bytes 1441824 | tf_op jit(solution)/shard_map/ppermute | solution.py:294
  90.0 0.0 copy-start.5
  90.0 0.0 collective-permute-done.3.kept_out2
  90.0 0.0 copy-done.7
  90.0 0.0 copy-start.13
  90.1 0.1 collective-permute-start.5
  90.2 0.0 copy-done.12
  90.2 1.0 copy-done.13
  91.2 0.0 collective-permute-start.6
  91.2 2.3 %collective-permute-done.5.last_in2 = bf16[704,1024]{1,0:T(8,128)(2,1)} collective-permute-done((bf16[704,1024]{1,0:T(8,128)(2,1)S(1)}, bf16[704,1024]{1,0:T(8,128)(2,1)}, u32[]{:S(2)}, u32[]{:S(2)}) %collective-permute-start.5) | collective-permute-done | bytes 1441824 | tf_op jit(solution)/shard_map/ppermute | solution.py:300
  93.5 10.2 %all-to-all-done.rows_hbm = bf16[128,8,1536]{2,1,0:T(8,128)(2,1)} async-done(((bf16[128,8,1536]{2,1,0:T(8,128)(2,1)}), bf16[128,8,1536]{2,1,0:T(8,128)(2,1)}, u32[]{:S(2)}, u32[]{:S(2)}) %all-to-all-start) | async-done | bytes 3145760 | tf_op jit(solution)/shard_map/all_to_all | solution.py:319
  103.7 0.0 copy-done.5
  103.7 15.3 %expert_first.1 = (f32[512,1024]{1,0:T(8,128)}, f32[512,1408]{1,0:T(8,128)}, bf16[512,1024]{1,0:T(8,128)(2,1)}) custom-call(bf16[128,8,1536]{2,1,0:T(8,128)(2,1)} %all-to-all-done.rows_hbm, bf16[704,1024]{1,0:T(8,128)(2,1)} %copy-done.7, bf16[704,1024]{1,0:T(8,128)(2,1)} %copy-done.12, bf16[704,1024]{1,0:T(8,128)(2,1)} %copy-done.6, ...), custom_call_target="tpu_custom_call" | custom-call | tf_op jit(solution)/shard_map/expert_first/pallas_call | solution.py:206
  119.0 0.0 collective-permute-done.6.last_out
  119.0 0.3 collective-permute-start.7
  119.3 3.4 %collective-permute-done.7.last_out2 = bf16[704,1024]{1,0:T(8,128)(2,1)S(1)} collective-permute-done((bf16[704,1024]{1,0:T(8,128)(2,1)}, bf16[704,1024]{1,0:T(8,128)(2,1)S(1)}, u32[]{:S(2)}, u32[]{:S(2)}) %collective-permute-start.7) | collective-permute-done | bytes 1441824 | tf_op jit(solution)/shard_map/ppermute | solution.py:303
  122.7 0.0 copy-start.11
  122.7 1.2 copy-done.11
  123.9 8.5 %expert_last.1 = bf16[64,2,8,512]{3,2,1,0:T(8,128)(2,1)} custom-call(bf16[512,1024]{1,0:T(8,128)(2,1)} %get-tuple-element.36.mult_ref, f32[512,1024]{1,0:T(8,128)} %get-tuple-element.38.partial_hbm, f32[512,1408]{1,0:T(8,128)} %get-tuple-element.39.ratio_hbm, bf16[704,1024]{1,0:T(8,128)(2,1)} %copy-done.5, ...), custom_call_target="tpu_custom_call" | custom-call | tf_op jit(solution)/shard_map/expert_last/pallas_call | solution.py:227
  132.4 0.0 copy-start
  132.4 0.0 copy-start.1
  132.4 0.0 copy-start.2
  132.4 0.0 copy-start.3
  132.4 0.0 copy-start.4
  132.5 38.5 %all_to_all.10 = bf16[128,8,512]{2,1,0:T(8,128)(2,1)S(1)} all-to-all(bf16[128,8,512]{2,1,0:T(8,128)(2,1)} %bitcast.36), channel_id=1, replica_groups={{0,1,2,3,8,9,10,11,16,17,18,19,24,25,26,27,32,33,34,35,40,41,42,43,48,4..., dimensions={0} | all-to-all | bytes 2097152 | tf_op jit(solution)/shard_map/all_to_all | solution.py:319
  170.9 0.0 copy-done
  170.9 0.0 copy-done.1
  170.9 0.0 copy-done.2
  170.9 0.0 copy-done.3
  170.9 0.0 copy-done.4
  171.0 1.6 combine.1
Async XLA Ops:
  0.0 3.8 %copy-start.9 = (bf16[2,1024,704]{1,2,0:T(8,128)(2,1)S(1)}, bf16[2,1024,704]{1,2,0:T(8,128)(2,1)}, u32[]{:S(2)}) copy-start(bf16[2,1024,704]{1,2,0:T(8,128)(2,1)} %param.23) | copy-start | bytes 8650756
  2.8 25.8 %collective-permute-start.1 = (bf16[704,1024]{1,0:T(8,128)(2,1)}, bf16[704,1024]{1,0:T(8,128)(2,1)}, u32[]{:S(2)}, u32[]{:S(2)}) collective-permute-start(bf16[704,1024]{1,0:T(8,128)(2,1)} %dynamic-slice_bitcast_fusion), channel_id=1, source_target_pairs={{0,5},{1,4},{2,1},{3,0},{4,7},{5,6},{6,3},{7,2},{8,13},{9,12},{10,... | collective-permute-start | bytes 4325384 | tf_op jit(solution)/shard_map/ppermute | solution.py:290
  5.1 43.1 %collective-permute-start = (bf16[704,1024]{1,0:T(8,128)(2,1)}, bf16[704,1024]{1,0:T(8,128)(2,1)}, u32[]{:S(2)}, u32[]{:S(2)}) collective-permute-start(bf16[704,1024]{1,0:T(8,128)(2,1)} %dynamic-slice_bitcast_fusion.1), channel_id=1, source_target_pairs={{0,5},{1,4},{2,1},{3,0},{4,7},{5,6},{6,3},{7,2},{8,13},{9,12},{10,... | collective-permute-start | bytes 4325384 | tf_op jit(solution)/shard_map/ppermute | solution.py:290
  14.2 34.0 %copy-start.8 = (bf16[2,1024,704]{1,2,0:T(8,128)(2,1)S(1)}, bf16[2,1024,704]{1,2,0:T(8,128)(2,1)}, u32[]{:S(2)}) copy-start(bf16[2,1024,704]{1,2,0:T(8,128)(2,1)} %param.24) | copy-start | bytes 8650756
  14.2 89.5 %all-to-all-start = ((bf16[128,8,1536]{2,1,0:T(8,128)(2,1)}), bf16[128,8,1536]{2,1,0:T(8,128)(2,1)}, u32[]{:S(2)}, u32[]{:S(2)}) async-start(bf16[128,8,1536]{2,1,0:T(8,128)(2,1)} %bitcast.37), calls=%async_computation | async-start | bytes 6291456 | tf_op jit(solution)/shard_map/all_to_all | solution.py:319
  48.2 2.9 %copy-start.10 = (bf16[2,1024,704]{1,2,0:T(8,128)(2,1)S(1)}, bf16[2,1024,704]{1,2,0:T(8,128)(2,1)}, u32[]{:S(2)}) copy-start(bf16[2,1024,704]{1,2,0:T(8,128)(2,1)} %param.23) | copy-start | bytes 8650756
  51.1 8.5 %copy-start.6 = (bf16[704,1024]{1,0:T(8,128)(2,1)}, bf16[704,1024]{1,0:T(8,128)(2,1)S(1)}, u32[]{:S(2)}) copy-start(bf16[704,1024]{1,0:T(8,128)(2,1)S(1)} %get-tuple-element.33.kept_out) | copy-start | bytes 4325380
  53.2 36.9 %copy-start.7 = (bf16[704,1024]{1,0:T(8,128)(2,1)}, bf16[704,1024]{1,0:T(8,128)(2,1)S(1)}, u32[]{:S(2)}) copy-start(bf16[704,1024]{1,0:T(8,128)(2,1)S(1)} %get-tuple-element.30.kept_in) | copy-start | bytes 4325380
  53.2 6.4 %collective-permute-start.2 = (bf16[704,1024]{1,0:T(8,128)(2,1)S(1)}, bf16[704,1024]{1,0:T(8,128)(2,1)S(1)}, u32[]{:S(2)}, u32[]{:S(2)}) collective-permute-start(bf16[704,1024]{1,0:T(8,128)(2,1)S(1)} %get-tuple-element.30.kept_in), channel_id=1, source_target_pairs={{0,4},{4,0},{8,12},{12,8},{16,20},{20,16},{24,28},{28,24},{32,36},... | collective-permute-start | bytes 4325384 | tf_op jit(solution)/shard_map/ppermute | solution.py:300
  56.7 33.3 %collective-permute-start.4 = (bf16[704,1024]{1,0:T(8,128)(2,1)S(1)}, bf16[704,1024]{1,0:T(8,128)(2,1)S(1)}, u32[]{:S(2)}, u32[]{:S(2)}) collective-permute-start(bf16[704,1024]{1,0:T(8,128)(2,1)S(1)} %get-tuple-element.43), channel_id=1, source_target_pairs={{0,1},{1,0},{2,5},{3,4},{4,3},{5,2},{6,7},{7,6},{8,9},{9,8},{10,13... | collective-permute-start | bytes 4325384 | tf_op jit(solution)/shard_map/ppermute | solution.py:294
  59.6 30.6 %copy-start.12 = (bf16[704,1024]{1,0:T(8,128)(2,1)}, bf16[704,1024]{1,0:T(8,128)(2,1)S(1)}, u32[]{:S(2)}) copy-start(bf16[704,1024]{1,0:T(8,128)(2,1)S(1)} %collective-permute-done.2.kept_in2) | copy-start | bytes 4325380
  59.6 30.5 %collective-permute-start.3 = (bf16[704,1024]{1,0:T(8,128)(2,1)S(1)}, bf16[704,1024]{1,0:T(8,128)(2,1)S(1)}, u32[]{:S(2)}, u32[]{:S(2)}) collective-permute-start(bf16[704,1024]{1,0:T(8,128)(2,1)S(1)} %get-tuple-element.33.kept_out), channel_id=1, source_target_pairs={{0,4},{4,0},{8,12},{12,8},{16,20},{20,16},{24,28},{28,24},{32,36},... | collective-permute-start | bytes 4325384 | tf_op jit(solution)/shard_map/ppermute | solution.py:300
  90.0 13.7 %copy-start.5 = (bf16[704,1024]{1,0:T(8,128)(2,1)}, bf16[704,1024]{1,0:T(8,128)(2,1)S(1)}, u32[]{:S(2)}) copy-start(bf16[704,1024]{1,0:T(8,128)(2,1)S(1)} %collective-permute-done.4.last_in) | copy-start | bytes 4325380
  90.0 1.1 copy-start.13
  90.1 3.4 %collective-permute-start.5 = (bf16[704,1024]{1,0:T(8,128)(2,1)S(1)}, bf16[704,1024]{1,0:T(8,128)(2,1)}, u32[]{:S(2)}, u32[]{:S(2)}) collective-permute-start(bf16[704,1024]{1,0:T(8,128)(2,1)S(1)} %collective-permute-done.4.last_in), channel_id=1, source_target_pairs={{0,4},{4,0},{8,12},{12,8},{16,20},{20,16},{24,28},{28,24},{32,36},... | collective-permute-start | bytes 4325384 | tf_op jit(solution)/shard_map/ppermute | solution.py:300
  91.2 27.8 %collective-permute-start.6 = (bf16[704,1024]{1,0:T(8,128)(2,1)}, bf16[704,1024]{1,0:T(8,128)(2,1)}, u32[]{:S(2)}, u32[]{:S(2)}) collective-permute-start(bf16[704,1024]{1,0:T(8,128)(2,1)} %get-tuple-element.41), channel_id=1, source_target_pairs={{0,1},{1,0},{2,5},{3,4},{4,3},{5,2},{6,7},{7,6},{8,9},{9,8},{10,13... | collective-permute-start | bytes 4325384 | tf_op jit(solution)/shard_map/ppermute | solution.py:294
  119.0 3.7 %collective-permute-start.7 = (bf16[704,1024]{1,0:T(8,128)(2,1)}, bf16[704,1024]{1,0:T(8,128)(2,1)S(1)}, u32[]{:S(2)}, u32[]{:S(2)}) collective-permute-start(bf16[704,1024]{1,0:T(8,128)(2,1)} %collective-permute-done.6.last_out), channel_id=1, source_target_pairs={{0,4},{4,0},{8,12},{12,8},{16,20},{20,16},{24,28},{28,24},{32,36},... | collective-permute-start | bytes 4325384 | tf_op jit(solution)/shard_map/ppermute | solution.py:303
  122.7 1.2 copy-start.11
  132.4 38.5 %copy-start = (f32[256,1024]{1,0:T(8,128)S(1)}, f32[256,1024]{1,0:T(8,128)}, u32[]{:S(2)}) copy-start(f32[256,1024]{1,0:T(8,128)} %get-tuple-element.24.layer_ref) | copy-start | bytes 3145732
  132.4 38.5 %copy-start.1 = (f32[256,128]{1,0:T(8,128)S(1)}, f32[256,128]{1,0:T(8,128)}, u32[]{:S(2)}) copy-start(f32[256,128]{1,0:T(8,128)} %get-tuple-element.23.scale_ref) | copy-start | bytes 393220
  132.4 38.5 %copy-start.2 = (f32[1024]{0:T(1024)S(1)}, f32[1024]{0:T(1024)}, u32[]{:S(2)}) copy-start(f32[1024]{0:T(1024)} %param.22) | copy-start | bytes 12292
  132.4 38.5 %copy-start.3 = (s32[1,1,256]{2,1,0:T(1,128)S(1)}, s32[1,1,256]{2,1,0:T(1,128)}, u32[]{:S(2)}) copy-start(s32[1,1,256]{2,1,0:T(1,128)} %param.19) | copy-start | bytes 3076
  132.4 38.5 %copy-start.4 = (s32[1,1,256]{2,1,0:T(1,128)S(1)}, s32[1,1,256]{2,1,0:T(1,128)}, u32[]{:S(2)}) copy-start(s32[1,1,256]{2,1,0:T(1,128)} %param.20) | copy-start | bytes 3076

commit v5 on v4

--- a/solution.py
+++ b/solution.py
@@ -165,10 +165,10 @@
 
 
 def last_kernel(
-    mult_ref, partial_hbm, ratio_hbm, last_in, last_in2, last_out, last_out2,
-    out_ref, partial_ref, ratio_ref, w_in_ref, w_out_ref, act_ref, sems,
+    mult_hbm, partial_hbm, ratio_hbm, last_in, last_in2, last_out, last_out2,
+    out_ref, mult_ref, partial_ref, ratio_ref, w_in_ref, w_out_ref, act_ref, sems,
 ):
-    n_rows, width = mult_ref.shape
+    n_rows, width = mult_hbm.shape
     half = width // 2
     n_tiles = n_rows // 4
     part_len = last_in.shape[0]
@@ -177,20 +177,25 @@
     def part(src, dst, i, sem):
         return pltpu.make_async_copy(src, dst.at[pl.ds(i * part_len, part_len)], sems.at[sem])
 
+    def ratio_part(lanes, sem):
+        return pltpu.make_async_copy(ratio_hbm.at[:, lanes], ratio_ref.at[:, lanes], sems.at[sem])
+
     copies = [
-        part(last_out, w_out_ref, 0, 0), pltpu.make_async_copy(ratio_hbm, ratio_ref, sems.at[1]),
-        part(last_out2, w_out_ref, 1, 2), part(last_in, w_in_ref, 0, 3), part(last_in2, w_in_ref, 1, 4),
-        pltpu.make_async_copy(partial_hbm, partial_ref, sems.at[5]),
+        part(last_out, w_out_ref, 0, 0), pltpu.make_async_copy(mult_hbm, mult_ref, sems.at[1]),
+        ratio_part(pl.ds(0, 512), 2), part(last_out2, w_out_ref, 1, 3), ratio_part(pl.ds(512, hidden - 512), 4),
+        part(last_in, w_in_ref, 0, 5), part(last_in2, w_in_ref, 1, 6),
+        pltpu.make_async_copy(partial_hbm, partial_ref, sems.at[7]),
     ]
     for copy in copies:
         copy.start()
-    for copy in copies[:2]:
+    for copy in copies[:3]:
         copy.wait()
     for i, cols in enumerate(hidden_blocks(hidden)):
-        if i == part_len // 256:
-            copies[2].wait()
+        if i == 2:
+            for copy in copies[3:5]:
+                copy.wait()
         act_ref[:, cols] = (ratio_ref[:, cols] * mm_nt(mult_ref[...], w_out_ref[cols, :])).astype(BF16)
-    for copy in copies[3:]:
+    for copy in copies[5:]:
         copy.wait()
     upper_rows = lax.broadcasted_iota(jnp.int32, (n_tiles // 2, 8, half), 1) < 4
     low = (partial_ref[:, :half] + mm(act_ref[...], w_in_ref[:, :half])).reshape(n_tiles // 2, 8, half)
@@ -226,15 +231,15 @@
     hidden = ratio.shape[1]
     return pl.pallas_call(
         last_kernel,
-        in_specs=[pl.BlockSpec(memory_space=pltpu.VMEM)] + [pl.BlockSpec(memory_space=pltpu.HBM)] * 6,
+        in_specs=[pl.BlockSpec(memory_space=pltpu.HBM)] * 6 + [pl.BlockSpec(memory_space=pltpu.VMEM)],
         out_specs=pl.BlockSpec(memory_space=pltpu.VMEM),
         out_shape=jax.ShapeDtypeStruct((n_rows // 8, 2, 8, width // 2), BF16),
         scratch_shapes=[
-            pltpu.VMEM((n_rows, width), F32), pltpu.VMEM((n_rows, hidden), F32),
+            pltpu.VMEM(mult.shape, BF16), pltpu.VMEM((n_rows, width), F32), pltpu.VMEM((n_rows, hidden), F32),
             pltpu.VMEM((hidden, width), BF16), pltpu.VMEM((hidden, width), BF16),
-            pltpu.VMEM((n_rows, hidden), BF16), pltpu.SemaphoreType.DMA((6,)),
+            pltpu.VMEM((n_rows, hidden), BF16), pltpu.SemaphoreType.DMA((8,)),
         ],
-        compiler_params=pltpu.CompilerParams(vmem_limit_bytes=62 << 20),
+        compiler_params=pltpu.CompilerParams(vmem_limit_bytes=58 << 20),
         name="expert_last",
     )(mult, partial, ratio, *weights)
 

time: 173 us -> 173 us (level)
  no operation moved by 1% of the time
where the time goes in v5:
time: 173 us
  waiting for transfers between devices  67.7 us (39%)
  blocking collectives  38.5 us (22%)
  Pallas kernels  32.5 us (19%)
  starting transfers between devices  21.7 us (13%)
  local copies, waits for them, and re-layouts  6.33 us (4%)
  other arithmetic  4.97 us (3%)
    all_to_all x1, blocking collectives, exchange(): lax.all_to_all(rows, axes, split_axis=0, concat_axis=0, axis_index_groups...  38.5 us
    ppermute x2, waiting for transfers between devices, expert_layer(): lax.ppermute(jnp.where(is_home, came, rest), axes, second_round)  29.5 us
    ppermute x2, waiting for transfers between devices, expert_layer(): lax.ppermute(lax.dynamic_index_in_dim(weights, first, 0, keepdims=False),...  19.5 us
    pallas_call x1, Pallas kernels, expert_first(): pl.pallas_call(first_kernel, in_specs=[pl.BlockSpec(memory_space=pltpu.HB...  15.3 us
    all_to_all x1, starting transfers between devices, exchange(): lax.all_to_all(rows, axes, split_axis=0, concat_axis=0, axis_index_groups...  14.4 us
    all_to_all x1, waiting for transfers between devices, exchange(): lax.all_to_all(rows, axes, split_axis=0, concat_axis=0, axis_index_groups...  10.2 us
    pallas_call x1, Pallas kernels, expert_last(): pl.pallas_call(last_kernel, in_specs=[pl.BlockSpec(memory_space=pltpu.HBM...  8.43 us
    pallas_call x1, Pallas kernels, prepare(): pl.pallas_call(prepare_kernel, in_specs=[pl.BlockSpec(memory_space=pltpu....  7.15 us
  transfers between devices with their start and end apart: 9, of which 6 were waited for; matrix products, arithmetic and copies ran while one was open for 4% of the time, Pallas kernels for 13%

profile of v5, /device:TPU:32, one launch (start us, length us, event | category | flops | bytes accessed | tf_op | source)
XLA Modules:
  0.0 172.6 jit_solution(15192903812302106941)
XLA Ops:
  0.0 0.0 copy-start.9
  0.0 2.8 %dynamic-slice_bitcast_fusion = bf16[704,1024]{1,0:T(8,128)(2,1)} fusion(bf16[2,1024,704]{1,2,0:T(8,128)(2,1)} %param.24, s32[]{:T(128)S(6)} %select_n.54), kind=kLoop, calls=%fused_computation.4 | loop fusion | bytes 2883588 | tf_op jit(solution)/shard_map/jit(dynamic_index_in_dim)/squeeze | solution.py:295
  2.8 1.0 collective-permute-start.1
  3.8 0.0 copy-done.9
  3.8 1.2 dynamic-slice_bitcast_fusion.1
  5.1 1.3 collective-permute-start
  7.0 7.2 %prepare.1 = (bf16[1024,1536]{1,0:T(8,128)(2,1)}, f32[256,1024]{1,0:T(8,128)}, f32[256,128]{1,0:T(8,128)}) custom-call(s32[1,1]{1,0:T(1,128)S(6)} %copy.14.length_ref, s32[1,256]{1,0:T(1,128)} %bitcast.32, s32[1,256]{1,0:T(1,128)} %bitcast.34, f32[1,256]{1,0:T(1,128)} %bitcast.45, f32[1,1024]{1,0:T(1,128)} %bitcast.30, bf16[256,1024]{1,0:T(8,128)(2,1)} %bitcast.40, ...), custom_call_target="tpu_custom_call" | custom-call | tf_op jit(solution)/shard_map/prepare/pallas_call | solution.py:92
  14.2 0.0 copy-start.8
  14.2 14.4 %all-to-all-start = ((bf16[128,8,1536]{2,1,0:T(8,128)(2,1)}), bf16[128,8,1536]{2,1,0:T(8,128)(2,1)}, u32[]{:S(2)}, u32[]{:S(2)}) async-start(bf16[128,8,1536]{2,1,0:T(8,128)(2,1)} %bitcast.37), calls=%async_computation | async-start | bytes 6291456 | tf_op jit(solution)/shard_map/all_to_all | solution.py:324
  28.6 0.0 collective-permute-done.1
  28.7 19.5 %collective-permute-done = bf16[704,1024]{1,0:T(8,128)(2,1)} collective-permute-done((bf16[704,1024]{1,0:T(8,128)(2,1)}, bf16[704,1024]{1,0:T(8,128)(2,1)}, u32[]{:S(2)}, u32[]{:S(2)}) %collective-permute-start) | collective-permute-done | bytes 1441824 | tf_op jit(solution)/shard_map/ppermute | solution.py:295
  48.2 0.0 copy-done.8
  48.2 0.0 copy-start.10
  48.2 2.9 %bitcast_select_fusion = (bf16[704,1024]{1,0:T(8,128)(2,1)}, bf16[704,1024]{1,0:T(8,128)(2,1)S(1)}) fusion(bf16[704,1024]{1,0:T(8,128)(2,1)} %collective-permute-done.1, pred[]{:T(512)S(6)} %eq.7, bf16[2,704,1024]{2,1,0:T(8,128)(2,1)S(1)} %bitcast.38, s32[]{:T(128)S(6)} %select_n.55), kind=kLoop, calls=%fused_computation | loop fusion | flops 1441792 | bytes 5767173 | tf_op jit(solution)/shard_map/jit(_where)/select_n | solution.py:299
  51.1 0.0 copy-done.10
  51.1 0.0 copy-start.6
  51.1 2.1 %bitcast_select_fusion.2 = (bf16[704,1024]{1,0:T(8,128)(2,1)S(1)}, bf16[704,1024]{1,0:T(8,128)(2,1)S(1)}) fusion(bf16[704,1024]{1,0:T(8,128)(2,1)} %collective-permute-done, pred[]{:T(512)S(6)} %eq.7, bf16[2,704,1024]{2,1,0:T(8,128)(2,1)S(1)} %bitcast.39, s32[]{:T(128)S(6)} %select_n.55), kind=kLoop, calls=%fused_computation.2 | loop fusion | flops 1441792 | bytes 5767173 | tf_op jit(solution)/shard_map/jit(_where)/select_n | solution.py:299
  53.2 0.0 copy-start.7
  53.2 3.5 %collective-permute-start.2 = (bf16[704,1024]{1,0:T(8,128)(2,1)S(1)}, bf16[704,1024]{1,0:T(8,128)(2,1)S(1)}, u32[]{:S(2)}, u32[]{:S(2)}) collective-permute-start(bf16[704,1024]{1,0:T(8,128)(2,1)S(1)} %get-tuple-element.30.kept_in), channel_id=1, source_target_pairs={{0,4},{4,0},{8,12},{12,8},{16,20},{20,16},{24,28},{28,24},{32,36},... | collective-permute-start | bytes 4325384 | tf_op jit(solution)/shard_map/ppermute | solution.py:305
  56.7 0.0 collective-permute-start.4
  56.7 2.8 %collective-permute-done.2.kept_in2 = bf16[704,1024]{1,0:T(8,128)(2,1)S(1)} collective-permute-done((bf16[704,1024]{1,0:T(8,128)(2,1)S(1)}, bf16[704,1024]{1,0:T(8,128)(2,1)S(1)}, u32[]{:S(2)}, u32[]{:S(2)}) %collective-permute-start.2) | collective-permute-done | bytes 1441824 | tf_op jit(solution)/shard_map/ppermute | solution.py:305
  59.6 0.0 copy-done.6
  59.6 0.0 copy-start.12
  59.6 1.0 collective-permute-start.3
  60.6 29.5 %collective-permute-done.4.last_in = bf16[704,1024]{1,0:T(8,128)(2,1)S(1)} collective-permute-done((bf16[704,1024]{1,0:T(8,128)(2,1)S(1)}, bf16[704,1024]{1,0:T(8,128)(2,1)S(1)}, u32[]{:S(2)}, u32[]{:S(2)}) %collective-permute-start.4) | collective-permute-done | bytes 1441824 | tf_op jit(solution)/shard_map/ppermute | solution.py:299
  90.0 0.0 copy-start.5
  90.0 0.0 collective-permute-done.3.kept_out2
  90.0 0.0 copy-done.7
  90.0 0.0 copy-start.13
  90.1 0.1 collective-permute-start.5
  90.2 0.0 copy-done.12
  90.2 1.0 copy-done.13
  91.2 0.0 collective-permute-start.6
  91.2 2.3 %collective-permute-done.5.last_in2 = bf16[704,1024]{1,0:T(8,128)(2,1)} collective-permute-done((bf16[704,1024]{1,0:T(8,128)(2,1)S(1)}, bf16[704,1024]{1,0:T(8,128)(2,1)}, u32[]{:S(2)}, u32[]{:S(2)}) %collective-permute-start.5) | collective-permute-done | bytes 1441824 | tf_op jit(solution)/shard_map/ppermute | solution.py:305
  93.5 10.2 %all-to-all-done.rows_hbm = bf16[128,8,1536]{2,1,0:T(8,128)(2,1)} async-done(((bf16[128,8,1536]{2,1,0:T(8,128)(2,1)}), bf16[128,8,1536]{2,1,0:T(8,128)(2,1)}, u32[]{:S(2)}, u32[]{:S(2)}) %all-to-all-start) | async-done | bytes 3145760 | tf_op jit(solution)/shard_map/all_to_all | solution.py:324
  103.7 0.0 copy-done.5
  103.7 15.3 %expert_first.1 = (f32[512,1024]{1,0:T(8,128)}, f32[512,1408]{1,0:T(8,128)}, bf16[512,1024]{1,0:T(8,128)(2,1)}) custom-call(bf16[128,8,1536]{2,1,0:T(8,128)(2,1)} %all-to-all-done.rows_hbm, bf16[704,1024]{1,0:T(8,128)(2,1)} %copy-done.7, bf16[704,1024]{1,0:T(8,128)(2,1)} %copy-done.12, bf16[704,1024]{1,0:T(8,128)(2,1)} %copy-done.6, ...), custom_call_target="tpu_custom_call" | custom-call | tf_op jit(solution)/shard_map/expert_first/pallas_call | solution.py:211
  119.0 0.0 collective-permute-done.6.last_out
  119.0 0.3 collective-permute-start.7
  119.3 3.4 %collective-permute-done.7.last_out2 = bf16[704,1024]{1,0:T(8,128)(2,1)S(1)} collective-permute-done((bf16[704,1024]{1,0:T(8,128)(2,1)}, bf16[704,1024]{1,0:T(8,128)(2,1)S(1)}, u32[]{:S(2)}, u32[]{:S(2)}) %collective-permute-start.7) | collective-permute-done | bytes 1441824 | tf_op jit(solution)/shard_map/ppermute | solution.py:308
  122.7 0.0 copy-start.11
  122.7 1.2 copy-done.11
  123.9 8.4 %expert_last.1 = bf16[64,2,8,512]{3,2,1,0:T(8,128)(2,1)} custom-call(bf16[512,1024]{1,0:T(8,128)(2,1)} %get-tuple-element.36.mult_hbm, f32[512,1024]{1,0:T(8,128)} %get-tuple-element.38.partial_hbm, f32[512,1408]{1,0:T(8,128)} %get-tuple-element.39.ratio_hbm, bf16[704,1024]{1,0:T(8,128)(2,1)} %copy-done.5, ...), custom_call_target="tpu_custom_call" | custom-call | tf_op jit(solution)/shard_map/expert_last/pallas_call | solution.py:232
  132.4 0.0 copy-start
  132.4 0.0 copy-start.1
  132.4 0.0 copy-start.2
  132.4 0.0 copy-start.3
  132.4 0.0 copy-start.4
  132.4 38.5 %all_to_all.10 = bf16[128,8,512]{2,1,0:T(8,128)(2,1)S(1)} all-to-all(bf16[128,8,512]{2,1,0:T(8,128)(2,1)} %bitcast.36), channel_id=1, replica_groups={{0,1,2,3,8,9,10,11,16,17,18,19,24,25,26,27,32,33,34,35,40,41,42,43,48,4..., dimensions={0} | all-to-all | bytes 2097152 | tf_op jit(solution)/shard_map/all_to_all | solution.py:324
  170.9 0.0 copy-done
  170.9 0.0 copy-done.1
  170.9 0.0 copy-done.2
  170.9 0.0 copy-done.3
  170.9 0.0 copy-done.4
  170.9 1.6 combine.1
Async XLA Ops:
  0.0 3.8 %copy-start.9 = (bf16[2,1024,704]{1,2,0:T(8,128)(2,1)S(1)}, bf16[2,1024,704]{1,2,0:T(8,128)(2,1)}, u32[]{:S(2)}) copy-start(bf16[2,1024,704]{1,2,0:T(8,128)(2,1)} %param.23) | copy-start | bytes 8650756
  2.8 25.8 %collective-permute-start.1 = (bf16[704,1024]{1,0:T(8,128)(2,1)}, bf16[704,1024]{1,0:T(8,128)(2,1)}, u32[]{:S(2)}, u32[]{:S(2)}) collective-permute-start(bf16[704,1024]{1,0:T(8,128)(2,1)} %dynamic-slice_bitcast_fusion), channel_id=1, source_target_pairs={{0,5},{1,4},{2,1},{3,0},{4,7},{5,6},{6,3},{7,2},{8,13},{9,12},{10,... | collective-permute-start | bytes 4325384 | tf_op jit(solution)/shard_map/ppermute | solution.py:295
  5.1 43.1 %collective-permute-start = (bf16[704,1024]{1,0:T(8,128)(2,1)}, bf16[704,1024]{1,0:T(8,128)(2,1)}, u32[]{:S(2)}, u32[]{:S(2)}) collective-permute-start(bf16[704,1024]{1,0:T(8,128)(2,1)} %dynamic-slice_bitcast_fusion.1), channel_id=1, source_target_pairs={{0,5},{1,4},{2,1},{3,0},{4,7},{5,6},{6,3},{7,2},{8,13},{9,12},{10,... | collective-permute-start | bytes 4325384 | tf_op jit(solution)/shard_map/ppermute | solution.py:295
  14.2 34.0 %copy-start.8 = (bf16[2,1024,704]{1,2,0:T(8,128)(2,1)S(1)}, bf16[2,1024,704]{1,2,0:T(8,128)(2,1)}, u32[]{:S(2)}) copy-start(bf16[2,1024,704]{1,2,0:T(8,128)(2,1)} %param.24) | copy-start | bytes 8650756
  14.2 89.5 %all-to-all-start = ((bf16[128,8,1536]{2,1,0:T(8,128)(2,1)}), bf16[128,8,1536]{2,1,0:T(8,128)(2,1)}, u32[]{:S(2)}, u32[]{:S(2)}) async-start(bf16[128,8,1536]{2,1,0:T(8,128)(2,1)} %bitcast.37), calls=%async_computation | async-start | bytes 6291456 | tf_op jit(solution)/shard_map/all_to_all | solution.py:324
  48.2 2.9 %copy-start.10 = (bf16[2,1024,704]{1,2,0:T(8,128)(2,1)S(1)}, bf16[2,1024,704]{1,2,0:T(8,128)(2,1)}, u32[]{:S(2)}) copy-start(bf16[2,1024,704]{1,2,0:T(8,128)(2,1)} %param.23) | copy-start | bytes 8650756
  51.1 8.5 %copy-start.6 = (bf16[704,1024]{1,0:T(8,128)(2,1)}, bf16[704,1024]{1,0:T(8,128)(2,1)S(1)}, u32[]{:S(2)}) copy-start(bf16[704,1024]{1,0:T(8,128)(2,1)S(1)} %get-tuple-element.33.kept_out) | copy-start | bytes 4325380
  53.2 36.9 %copy-start.7 = (bf16[704,1024]{1,0:T(8,128)(2,1)}, bf16[704,1024]{1,0:T(8,128)(2,1)S(1)}, u32[]{:S(2)}) copy-start(bf16[704,1024]{1,0:T(8,128)(2,1)S(1)} %get-tuple-element.30.kept_in) | copy-start | bytes 4325380
  53.2 6.4 %collective-permute-start.2 = (bf16[704,1024]{1,0:T(8,128)(2,1)S(1)}, bf16[704,1024]{1,0:T(8,128)(2,1)S(1)}, u32[]{:S(2)}, u32[]{:S(2)}) collective-permute-start(bf16[704,1024]{1,0:T(8,128)(2,1)S(1)} %get-tuple-element.30.kept_in), channel_id=1, source_target_pairs={{0,4},{4,0},{8,12},{12,8},{16,20},{20,16},{24,28},{28,24},{32,36},... | collective-permute-start | bytes 4325384 | tf_op jit(solution)/shard_map/ppermute | solution.py:305
  56.7 33.3 %collective-permute-start.4 = (bf16[704,1024]{1,0:T(8,128)(2,1)S(1)}, bf16[704,1024]{1,0:T(8,128)(2,1)S(1)}, u32[]{:S(2)}, u32[]{:S(2)}) collective-permute-start(bf16[704,1024]{1,0:T(8,128)(2,1)S(1)} %get-tuple-element.43), channel_id=1, source_target_pairs={{0,1},{1,0},{2,5},{3,4},{4,3},{5,2},{6,7},{7,6},{8,9},{9,8},{10,13... | collective-permute-start | bytes 4325384 | tf_op jit(solution)/shard_map/ppermute | solution.py:299
  59.6 30.6 %copy-start.12 = (bf16[704,1024]{1,0:T(8,128)(2,1)}, bf16[704,1024]{1,0:T(8,128)(2,1)S(1)}, u32[]{:S(2)}) copy-start(bf16[704,1024]{1,0:T(8,128)(2,1)S(1)} %collective-permute-done.2.kept_in2) | copy-start | bytes 4325380
  59.6 30.5 %collective-permute-start.3 = (bf16[704,1024]{1,0:T(8,128)(2,1)S(1)}, bf16[704,1024]{1,0:T(8,128)(2,1)S(1)}, u32[]{:S(2)}, u32[]{:S(2)}) collective-permute-start(bf16[704,1024]{1,0:T(8,128)(2,1)S(1)} %get-tuple-element.33.kept_out), channel_id=1, source_target_pairs={{0,4},{4,0},{8,12},{12,8},{16,20},{20,16},{24,28},{28,24},{32,36},... | collective-permute-start | bytes 4325384 | tf_op jit(solution)/shard_map/ppermute | solution.py:305
  90.0 13.7 %copy-start.5 = (bf16[704,1024]{1,0:T(8,128)(2,1)}, bf16[704,1024]{1,0:T(8,128)(2,1)S(1)}, u32[]{:S(2)}) copy-start(bf16[704,1024]{1,0:T(8,128)(2,1)S(1)} %collective-permute-done.4.last_in) | copy-start | bytes 4325380
  90.0 1.1 copy-start.13
  90.1 3.4 %collective-permute-start.5 = (bf16[704,1024]{1,0:T(8,128)(2,1)S(1)}, bf16[704,1024]{1,0:T(8,128)(2,1)}, u32[]{:S(2)}, u32[]{:S(2)}) collective-permute-start(bf16[704,1024]{1,0:T(8,128)(2,1)S(1)} %collective-permute-done.4.last_in), channel_id=1, source_target_pairs={{0,4},{4,0},{8,12},{12,8},{16,20},{20,16},{24,28},{28,24},{32,36},... | collective-permute-start | bytes 4325384 | tf_op jit(solution)/shard_map/ppermute | solution.py:305
  91.2 27.8 %collective-permute-start.6 = (bf16[704,1024]{1,0:T(8,128)(2,1)}, bf16[704,1024]{1,0:T(8,128)(2,1)}, u32[]{:S(2)}, u32[]{:S(2)}) collective-permute-start(bf16[704,1024]{1,0:T(8,128)(2,1)} %get-tuple-element.41), channel_id=1, source_target_pairs={{0,1},{1,0},{2,5},{3,4},{4,3},{5,2},{6,7},{7,6},{8,9},{9,8},{10,13... | collective-permute-start | bytes 4325384 | tf_op jit(solution)/shard_map/ppermute | solution.py:299
  119.0 3.7 %collective-permute-start.7 = (bf16[704,1024]{1,0:T(8,128)(2,1)}, bf16[704,1024]{1,0:T(8,128)(2,1)S(1)}, u32[]{:S(2)}, u32[]{:S(2)}) collective-permute-start(bf16[704,1024]{1,0:T(8,128)(2,1)} %collective-permute-done.6.last_out), channel_id=1, source_target_pairs={{0,4},{4,0},{8,12},{12,8},{16,20},{20,16},{24,28},{28,24},{32,36},... | collective-permute-start | bytes 4325384 | tf_op jit(solution)/shard_map/ppermute | solution.py:308
  122.7 1.2 copy-start.11
  132.4 38.5 %copy-start = (f32[256,1024]{1,0:T(8,128)S(1)}, f32[256,1024]{1,0:T(8,128)}, u32[]{:S(2)}) copy-start(f32[256,1024]{1,0:T(8,128)} %get-tuple-element.24.layer_ref) | copy-start | bytes 3145732
  132.4 38.5 %copy-start.1 = (f32[256,128]{1,0:T(8,128)S(1)}, f32[256,128]{1,0:T(8,128)}, u32[]{:S(2)}) copy-start(f32[256,128]{1,0:T(8,128)} %get-tuple-element.23.scale_ref) | copy-start | bytes 393220
  132.4 38.5 %copy-start.2 = (f32[1024]{0:T(1024)S(1)}, f32[1024]{0:T(1024)}, u32[]{:S(2)}) copy-start(f32[1024]{0:T(1024)} %param.22) | copy-start | bytes 12292
  132.4 38.5 %copy-start.3 = (s32[1,1,256]{2,1,0:T(1,128)S(1)}, s32[1,1,256]{2,1,0:T(1,128)}, u32[]{:S(2)}) copy-start(s32[1,1,256]{2,1,0:T(1,128)} %param.19) | copy-start | bytes 3076
  132.4 38.5 %copy-start.4 = (s32[1,1,256]{2,1,0:T(1,128)S(1)}, s32[1,1,256]{2,1,0:T(1,128)}, u32[]{:S(2)}) copy-start(s32[1,1,256]{2,1,0:T(1,128)} %param.20) | copy-start | bytes 3076
